TPU v7x, 32 devices: a whole 2x2x4 slice. The times are simulated.
32 devices in a mesh: fsdp: 32 (over z, y, x, core).
Axes of the slice: x: 2, y: 2, z: 4, core: 2. Of those that a mesh axis runs over, the one named last changes fastest.
Arguments:
- tokens: bfloat16 [32768, 1024], P('fsdp'), may hold values from -5 to 5
- cotangent: bfloat16 [32768, 1024], P('fsdp'), may hold values from -6 to 6
- segment: int32 [32768], P('fsdp'), may hold values from -1 to 511, as said below
- w_qkv: bfloat16 [3072, 1024], P('fsdp'), may hold values from -0.09375 to 0.09375
- w_attn_out: bfloat16 [1024, 1024], P('fsdp'), may hold values from -0.75 to 0.75
- w_in: bfloat16 [5248, 1024], P('fsdp'), may hold values from -0.1875 to 0.1875
- w_ff_out: bfloat16 [1024, 2624], P('fsdp'), may hold values from -0.125 to 0.125
- norm_one: bfloat16 [1024], P('fsdp'), may hold values from 0.25 to 1.75
- norm_two: bfloat16 [1024], P('fsdp'), may hold values from 0.25 to 1.75
Outputs:
- output: bfloat16 [32768, 1024], P('fsdp')
- grad_tokens: float32 [32768, 1024], P('fsdp')
- grad_qkv: float32 [3072, 1024], P('fsdp')
- grad_attn_out: float32 [1024, 1024], P('fsdp')
- grad_in: float32 [5248, 1024], P('fsdp')
- grad_ff_out: float32 [1024, 2624], P('fsdp')
- grad_norm_one: float32 [1024], P('fsdp')
- grad_norm_two: float32 [1024], P('fsdp')
Inputs may be any that keep to these rules, and one draw needn't show every extreme that they name: `segment`: within each block of 1024 slots the non-negative values start at 0 and rise by one at each new sequence, and the -1 slots, if any, come last; each run of one value other than -1 is at most 1024 long and at least 2 long unless -1 slots follow it; some run is exactly 1024 long, and some block reaches the largest value.
All inputs are finite; a program needn't handle non-finite values.
Results may differ from a plain program's by a relative error of at most 0.0084.
Values may be sent and summed in bfloat16 or wider, within the bound.
No kernel may reach another device: no remote copies, remote signals or barrier semaphores. Data moves between devices by JAX's collectives and lax.ppermute only.
A program may use at most 320 MiB of HBM per device.

v0:
```python
import functools
import math

import jax
import jax.numpy as jnp
from jax import lax
from jax.experimental import pallas as pl
from jax.experimental.pallas import tpu as pltpu
from jax.sharding import PartitionSpec as P

HD = 64
EPS = 1e-05
THETA = 160000.0
NEG = -1e30
LANES = 128
F32 = jnp.float32
BF16 = jnp.bfloat16
VMEM_BYTES = 62 << 20


def dot_nt(left, right):
    return lax.dot_general(left, right, (((1,), (1,)), ((), ())), preferred_element_type=F32)


def dot_nn(left, right):
    return lax.dot_general(left, right, (((1,), (0,)), ((), ())), preferred_element_type=F32)


def dot_tn(left, right):
    return lax.dot_general(left, right, (((0,), (0,)), ((), ())), preferred_element_type=F32)


def call(kernel, *, name, grid, in_specs, out_specs, out_shape, scratch=(), flops=0, nbytes=0, aliases=None):
    return pl.pallas_call(
        kernel,
        name=name,
        grid=grid,
        in_specs=in_specs,
        out_specs=out_specs,
        out_shape=out_shape,
        scratch_shapes=list(scratch),
        input_output_aliases=aliases or {},
        compiler_params=pltpu.CompilerParams(
            dimension_semantics=("arbitrary",) * len(grid), vmem_limit_bytes=VMEM_BYTES
        ),
        cost_estimate=pl.CostEstimate(flops=flops, transcendentals=0, bytes_accessed=nbytes),
    )


def sds(shape, dtype):
    return jax.ShapeDtypeStruct(shape, dtype)


def whole(shape, once=False):
    zeros = (0,) * len(shape)
    mode = dict(pipeline_mode=pl.Buffered(1)) if once else {}
    return pl.BlockSpec(shape, lambda *_: zeros, **mode)


def normalise(field):
    centre = jnp.mean(field, axis=-1, keepdims=True)
    centered = field - centre
    variance = jnp.mean(centered * centered, axis=-1, keepdims=True)
    inverse = lax.rsqrt(variance + EPS)
    return centered * inverse, inverse


def minus_row(field, row):
    return (field.reshape(-1, *row.shape) - row[None]).reshape(field.shape)


def swap_halves(field):
    lane = lax.broadcasted_iota(jnp.int32, field.shape, 1)
    first = (lane & (HD - 1)) < HD // 2
    return jnp.where(
        first, pltpu.roll(field, LANES - HD // 2, 1), pltpu.roll(field, HD // 2, 1)
    )


def fetch(weights, at, rows, target, sem, group=None):
    order_ref, pieces = weights
    i = 0
    for piece in pieces:
        for slot in range(piece.shape[0]):
            device = order_ref[i]
            start = pl.multiple_of(device * rows, rows)
            pltpu.make_async_copy(
                piece.at[slot, pl.ds(at, rows), :],
                target.at[pl.ds(start, rows), :],
                sem if group is None else sem.at[device // group],
            ).start()
            i += 1


def arrive(target, sem):
    pltpu.make_async_copy(target, target, sem).wait()


def grouping(weights, group):
    devices = weights[0].shape[0]
    return (group, devices // group) if devices % group == 0 else (devices, 1)


def arrive_in_time(target, sem, rows, groups, block, step):
    for g in groups:
        @pl.when(step == (g - groups[0]) * rows // block)
        def _(g=g):
            arrive(target.at[pl.ds(g * rows, rows), :], sem.at[g])


def fetching_call(
    kernel, weights, *, name, grid, in_specs, out_specs, out_shape, scratch=(), flops=0, nbytes=0
):
    number = len(weights)

    def run(*refs):
        orders, rest, sets = refs[:number], refs[number:], []
        for order, (_, pieces) in zip(orders, weights, strict=True):
            sets.append((order, rest[: len(pieces)]))
            rest = rest[len(pieces) :]
        kernel(*sets, *rest)

    pieces = [piece for _, some in weights for piece in some]
    made = pl.pallas_call(
        run,
        name=name,
        grid_spec=pltpu.PrefetchScalarGridSpec(
            num_scalar_prefetch=number,
            grid=grid,
            in_specs=[pl.BlockSpec(memory_space=pl.ANY)] * len(pieces) + in_specs,
            out_specs=out_specs,
            scratch_shapes=list(scratch),
        ),
        out_shape=out_shape,
        compiler_params=pltpu.CompilerParams(
            dimension_semantics=("arbitrary",) * len(grid), vmem_limit_bytes=VMEM_BYTES
        ),
        cost_estimate=pl.CostEstimate(flops=flops, transcendentals=0, bytes_accessed=nbytes),
    )
    return lambda *args: made(*[order for order, _ in weights], *pieces, *args)


def unpack_gains(rows_ref, number, out_ref):
    total, width = rows_ref.shape
    devices = total // 8
    owner = lax.broadcasted_iota(jnp.int32, (devices, total), 0)
    row = lax.broadcasted_iota(jnp.int32, (devices, total), 1)
    found = dot_nn((row == owner * 8).astype(BF16), rows_ref[:, :LANES]).astype(BF16)
    place_in = lax.broadcasted_iota(jnp.int32, (LANES, width), 0)
    lane = lax.broadcasted_iota(jnp.int32, (LANES, width), 1) & (number - 1)
    first = lax.broadcasted_iota(jnp.int32, (devices, width), 0) * number
    column = lax.broadcasted_iota(jnp.int32, (devices, width), 1)
    mine = (column >= first) & (column < first + number)
    for which in range(2):
        tiled = dot_nn(found, (place_in == lane + which * number).astype(BF16))
        out_ref[which : which + 1, :] = jnp.sum(jnp.where(mine, tiled, 0.0), axis=0, keepdims=True)


def project_kernel(rope_blocks, query_blocks, rows, given, group, groups, weights, tok_ref, cos_ref, sin_ref, *refs):
    if given:
        gains_in, out_ref, hid_ref, gains_ref, w_ref, sem = refs
    else:
        out_ref, hid_ref, gains_ref, w_ref, sem, rows_ref, rows_sem = refs
    step = pl.program_id(0)
    block = out_ref.shape[1]

    @pl.when(step == 0)
    def _():
        if given:
            gains_ref[...] = gains_in[...]
        else:
            fetch(weights, rows, 8, rows_ref, rows_sem)
        fetch(weights, 0, rows, w_ref, sem, group)
        if not given:
            arrive(rows_ref, rows_sem)
            unpack_gains(rows_ref, w_ref.shape[1] * 8 // rows_ref.shape[0], gains_ref)
        normed, _ = normalise(tok_ref[...].astype(F32))
        hid_ref[...] = (normed * gains_ref[:1, :]).astype(BF16)

    arrive_in_time(w_ref, sem, group * rows, range(groups), block, step)
    w_block = w_ref[pl.ds(pl.multiple_of(step * block, block), block), :]
    some = 256

    @pl.when(step < rope_blocks)
    def _():
        scale = jnp.where(step < query_blocks, 1.0 / math.sqrt(HD), 1.0).astype(F32)
        for r in range(hid_ref.shape[0] // some):
            at = slice(r * some, (r + 1) * some)
            acc = dot_nt(hid_ref[at, :], w_block)
            cosine, sine = cos_ref[at, :] * scale, sin_ref[at, :] * scale
            for s in range(block // LANES):
                part = acc[:, s * LANES : (s + 1) * LANES]
                out_ref[at, s * LANES : (s + 1) * LANES] = (part * cosine + swap_halves(part) * sine).astype(BF16)

    @pl.when(step >= rope_blocks)
    def _():
        for r in range(hid_ref.shape[0] // some):
            at = slice(r * some, (r + 1) * some)
            out_ref[at, :] = dot_nt(hid_ref[at, :], w_block).astype(BF16)


def project(tokens, cosine, sine, weights, rows, gains=None):
    count, width = tokens.shape
    total = 3 * width
    block = 512
    given = gains is not None
    group, groups = grouping(weights, 4)
    own = [] if given else [pltpu.VMEM((weights[0].shape[0] * 8, width), BF16), pltpu.SemaphoreType.DMA]
    return fetching_call(
        functools.partial(project_kernel, 2 * width // block, width // block, rows, given, group, groups),
        [weights],
        name="norm_project",
        grid=(total // block,),
        in_specs=[whole((count, width)), whole((count, LANES)), whole((count, LANES))]
        + [whole((2, width))] * given,
        out_specs=[
            pl.BlockSpec((count, block), lambda j, *_: (0, j)),
            whole((count, width)),
            whole((2, width)),
        ],
        out_shape=[sds((count, total), BF16), sds((count, width), BF16), sds((2, width), F32)],
        scratch=[pltpu.VMEM((total, width), BF16), pltpu.SemaphoreType.DMA((groups,))] + own,
        flops=2 * count * width * total,
        nbytes=2 * (2 * count * width + total * width + total * count),
    )(tokens, cosine, sine, *([gains] if given else []))


def attend_kernel(q_ref, k_ref, v_ref, segc_ref, segr_ref, out_ref, lse_ref, vt_ref, ot_ref):
    count = q_ref.shape[0]
    vt_ref[...] = v_ref[...].T
    keys, query = k_ref[...], q_ref[...]
    lane = lax.broadcasted_iota(jnp.int32, query.shape, 1)
    allowed = jnp.concatenate([segc_ref[...]] * (count // LANES), axis=1) == segr_ref[...]
    for h in range(2):
        picked = jnp.where((lane >= h * HD) & (lane < (h + 1) * HD), query, jnp.zeros_like(query))
        scores = jnp.where(allowed, dot_nt(keys, picked), NEG)
        top = jnp.max(scores, axis=0, keepdims=True)
        powers = jnp.exp(scores - top)
        total = jnp.sum(powers, axis=0, keepdims=True)
        lse_ref[0, h : h + 1, :] = top + jnp.log(total)
        ot_ref[h * HD : (h + 1) * HD, :] = dot_nn(vt_ref[h * HD : (h + 1) * HD, :], powers.astype(BF16)) / total
    out_ref[...] = ot_ref[...].T.astype(BF16)


def attend(qkv, seg_column, seg_row, width, first, number, before=None):
    count = qkv.shape[0]
    pairs = width // LANES
    kept = () if before is None else tuple(before)

    def kernel(*refs):
        attend_kernel(*refs[:5], *refs[5 + len(kept) :])

    tall = lambda offset: pl.BlockSpec((count, LANES), lambda p: (0, offset + first + p))
    return call(
        kernel,
        name="attend",
        grid=(number,),
        in_specs=[tall(0), tall(pairs), tall(2 * pairs), whole((count, LANES)), whole((1, count))]
        + [pl.BlockSpec(memory_space=pl.ANY)] * len(kept),
        out_specs=[tall(0), pl.BlockSpec((1, 2, count), lambda p: (first + p, 0, 0))],
        out_shape=[sds((count, width), BF16), sds((pairs, 2, count), F32)],
        scratch=[pltpu.VMEM((LANES, count), BF16), pltpu.VMEM((LANES, count), F32)],
        flops=16 * count * count * LANES * number,
        nbytes=2 * 4 * count * LANES * number,
        aliases={5: 0, 6: 1} if kept else None,
    )(qkv, qkv, qkv, seg_column, seg_row, *kept)


def attend_back_kernel(
    chunk, q_ref, k_ref, v_ref, o_ref, g_ref, lse_ref, segc_ref, segr_ref, cos_ref, sin_ref,
    out_ref, kt_ref, dk_ref, dv_ref, dqt_ref, delta_ref, total_ref,
):
    count = q_ref.shape[0]
    kt_ref[...] = k_ref[...].T
    keys, values = k_ref[...], v_ref[...]
    product = (g_ref[...].astype(F32) * o_ref[...].astype(F32)).T
    for h in range(2):
        row = jnp.sum(product[h * HD : (h + 1) * HD, :], axis=0, keepdims=True)
        delta_ref[h] = jnp.broadcast_to(row, (8, count))
        total_ref[h] = jnp.broadcast_to(lse_ref[0, h : h + 1, :], (8, count))
    lane = lax.broadcasted_iota(jnp.int32, (chunk, LANES), 1)
    upper = lax.broadcasted_iota(jnp.int32, (LANES, chunk), 0) < HD
    for c in range(count // chunk):
        at = slice(c * chunk, (c + 1) * chunk)
        query, grad = q_ref[at, :], g_ref[at, :]
        allowed = jnp.concatenate([segc_ref[...]] * (chunk // LANES), axis=1) == segr_ref[:, at]
        grads = []
        for h in range(2):
            mine = (lane >= h * HD) & (lane < (h + 1) * HD)
            query_h = jnp.where(mine, query, jnp.zeros_like(query))
            grad_h = jnp.where(mine, grad, jnp.zeros_like(grad))
            scores = jnp.where(allowed, dot_nt(keys, query_h), NEG)
            weights = jnp.exp(minus_row(scores, total_ref[h, :, at]))
            grad_value = dot_nn(weights.astype(BF16), grad_h)
            spread = minus_row(dot_nt(values, grad_h), delta_ref[h, :, at])
            grad_scores = (weights * spread).astype(BF16)
            grads.append((dot_nn(grad_scores, query_h), grad_value, dot_nn(kt_ref[...], grad_scores)))
        (key_0, value_0, query_0), (key_1, value_1, query_1) = grads
        dqt_ref[:, at] = jnp.where(upper, query_0, query_1)
        if c == 0:
            dk_ref[...] = key_0 + key_1
            dv_ref[...] = value_0 + value_1
        else:
            dk_ref[...] += key_0 + key_1
            dv_ref[...] += value_0 + value_1

    cosine, sine = cos_ref[...], sin_ref[...]
    grad_query = dqt_ref[...].T * (1.0 / math.sqrt(HD))
    out_ref[0] = (grad_query * cosine - swap_halves(grad_query) * sine).astype(BF16)
    grad_key = dk_ref[...]
    out_ref[1] = (grad_key * cosine - swap_halves(grad_key) * sine).astype(BF16)
    out_ref[2] = dv_ref[...].astype(BF16)


def attend_back(qkv, attn_out, grad_heads, lse, seg_column, seg_row, cosine, sine, first, number, before=None):
    count, width = attn_out.shape
    pairs = width // LANES
    chunk = 256
    kept = () if before is None else (before,)

    def kernel(*refs):
        attend_back_kernel(chunk, *refs[:10], *refs[10 + len(kept) :])

    tall = lambda offset: pl.BlockSpec((count, LANES), lambda p: (0, offset + first + p))
    return call(
        kernel,
        name="attend_back",
        grid=(number,),
        in_specs=[
            tall(0),
            tall(pairs),
            tall(2 * pairs),
            tall(0),
            tall(0),
            pl.BlockSpec((1, 2, count), lambda p: (first + p, 0, 0)),
            whole((count, LANES)),
            whole((1, count)),
            whole((count, LANES)),
            whole((count, LANES)),
        ]
        + [pl.BlockSpec(memory_space=pl.ANY)] * len(kept),
        out_specs=pl.BlockSpec((3, count, LANES), lambda p: (0, 0, first + p)),
        out_shape=sds((3, count, width), BF16),
        scratch=[
            pltpu.VMEM((LANES, count), BF16),
            pltpu.VMEM((count, LANES), F32),
            pltpu.VMEM((count, LANES), F32),
            pltpu.VMEM((LANES, count), F32),
            pltpu.VMEM((2, 8, count), F32),
            pltpu.VMEM((2, 8, count), F32),
        ],
        flops=40 * count * count * LANES * number,
        nbytes=2 * 8 * count * LANES * number,
        aliases={10: 0} if kept else None,
    )(qkv, qkv, qkv, attn_out, grad_heads, lse, seg_column, seg_row, cosine, sine, *kept)


def ffn_kernel(
    rows_in, rows_out, rows_ff, group, groups, weights_in, weights_ff,
    tok_ref, attn_ref, cot_ref, gain_ref,
    resid_ref, mixed_ref, mid_ref, heads_ref, g_attn_ref, gnorm_ref, g_in_ref, g_out_ref,
    hid_ref, cot_t_ref, w_attn_ref, w_in_ref, w_ff_ref, sem_attn, sem_in, sem_ff,
):
    step = pl.program_id(0)
    count = resid_ref.shape[0]
    block = g_out_ref.shape[1]
    units = w_in_ref.shape[0] // 2
    width = hid_ref.shape[1]
    some = 256

    @pl.when(step == 0)
    def _():
        fetch(weights_in, rows_in, rows_out, w_attn_ref, sem_attn)
        fetch(weights_ff, 0, rows_ff, w_ff_ref.at[0], sem_ff.at[0])
        fetch(weights_in, 0, rows_in, w_in_ref, sem_in, group)
        for b in range(1, w_ff_ref.shape[0]):
            fetch(weights_ff, b * rows_ff, rows_ff, w_ff_ref.at[b], sem_ff.at[b])
        cot_t_ref[...] = cot_ref[...].T
        mid_ref[...] = jnp.zeros_like(mid_ref)
        arrive(w_attn_ref, sem_attn)
        for i in range(count // some):
            at = slice(i * some, (i + 1) * some)
            resid = tok_ref[at, :].astype(F32) + dot_nt(attn_ref[at, :], w_attn_ref[...])
            resid_ref[at, :] = resid
            normed, _ = normalise(resid)
            hid_ref[at, :] = (normed * gain_ref[1:, :]).astype(BF16)

    half = max(groups // 2, 1)
    for some_groups in (range(half), range(half, groups)):
        if some_groups:
            arrive_in_time(w_in_ref, sem_in, group * rows_in, some_groups, block, step)
    for b in range(w_ff_ref.shape[0]):
        pl.when(step == b * width // block)(functools.partial(arrive, w_ff_ref.at[b], sem_ff.at[b]))
    hidden = hid_ref[...]
    w_pre = w_in_ref[pl.ds(pl.multiple_of(step * block, block), block), :]
    w_gate = w_in_ref[pl.ds(pl.multiple_of(units + step * block, block), block), :]
    per = width // block
    w_out = w_ff_ref[step // per, :, pl.ds(pl.multiple_of(step % per * block, block), block)]
    pre = dot_nt(hidden, w_pre)
    gate = dot_nt(hidden, w_gate)
    grad_mixed = dot_nn(cot_ref[...], w_out)
    cdf = 0.5 * (1.0 + lax.erf(pre * 0.7071067811865476))
    density = jnp.exp(-0.5 * pre * pre) * 0.3989422804014327
    gelu = pre * cdf
    mixed = (gelu * gate).astype(BF16)
    mixed_ref[...] = mixed
    g_out_ref[...] = dot_nn(cot_t_ref[...], mixed).astype(BF16)
    grad_pre = (grad_mixed * gate * (cdf + pre * density)).astype(BF16)
    grad_gate = (grad_mixed * gelu).astype(BF16)
    g_in_ref[0] = dot_tn(grad_pre, hidden).astype(BF16)
    g_in_ref[1] = dot_tn(grad_gate, hidden).astype(BF16)
    mid_ref[...] += dot_nn(grad_pre, w_pre) + dot_nn(grad_gate, w_gate)

    @pl.when(step == pl.num_programs(0) - 1)
    def _():
        gnorm = jnp.zeros_like(gnorm_ref)
        for i in range(count // some):
            at = slice(i * some, (i + 1) * some)
            resid = resid_ref[at, :]
            normed, inverse = normalise(resid)
            grad = mid_ref[at, :]
            gnorm += jnp.sum(grad * normed, axis=0, keepdims=True)
            hat = grad * gain_ref[1:, :]
            first = jnp.mean(hat, axis=-1, keepdims=True)
            second = jnp.mean(hat * normed, axis=-1, keepdims=True)
            mid = cot_ref[at, :].astype(F32) + inverse * (hat - first - normed * second)
            mid_ref[at, :] = mid
            low = mid.astype(BF16)
            cot_t_ref[at, :] = low
            heads_ref[at, :] = dot_nn(low, w_attn_ref[...]).astype(BF16)
        gnorm_ref[...] = gnorm
        for i in range(width // some):
            at = slice(i * some, (i + 1) * some)
            g_attn_ref[at, :] = dot_tn(cot_t_ref[:, at], attn_ref[...]).astype(BF16)


def ffn(tokens, attn_out, cotangent, gains, w_in, w_ff, units, rows_in, rows_out, rows_ff):
    count, width = tokens.shape
    block = 256
    spans = -(-units // width)
    group, groups = grouping(w_in, 2)
    once = whole((count, width), once=True)
    return fetching_call(
        functools.partial(ffn_kernel, rows_in, rows_out, rows_ff, group, groups),
        [w_in, w_ff],
        name="ffn_forward_backward",
        grid=(units // block,),
        in_specs=[once, once, once, whole((2, width))],
        out_specs=[
            once,
            pl.BlockSpec((count, block), lambda j, *_: (0, j)),
            once,
            once,
            whole((width, width), once=True),
            whole((1, width)),
            pl.BlockSpec((2, block, width), lambda j, *_: (0, j, 0)),
            pl.BlockSpec((width, block), lambda j, *_: (0, j)),
        ],
        out_shape=[
            sds((count, width), F32),
            sds((count, units), BF16),
            sds((count, width), F32),
            sds((count, width), BF16),
            sds((width, width), BF16),
            sds((1, width), F32),
            sds((2, units, width), BF16),
            sds((width, units), BF16),
        ],
        scratch=[
            pltpu.VMEM((count, width), BF16),
            pltpu.VMEM((width, count), BF16),
            pltpu.VMEM((width, width), BF16),
            pltpu.VMEM((2 * units, width), BF16),
            pltpu.VMEM((spans, width, width), BF16),
            pltpu.SemaphoreType.DMA,
            pltpu.SemaphoreType.DMA((groups,)),
            pltpu.SemaphoreType.DMA((spans,)),
        ],
        flops=16 * count * width * units,
        nbytes=2 * (10 * count * width + 6 * units * width),
    )(tokens, attn_out, cotangent, gains)


def ffn_out_kernel(rows_ff, weights, resid_ref, mixed_ref, out_ref, w_ref, sem):
    @pl.when(pl.program_id(0) == 0)
    def _():
        for b in range(w_ref.shape[0]):
            fetch(weights, b * rows_ff, rows_ff, w_ref.at[b], sem.at[b])

    units, width = mixed_ref.shape[1], out_ref.shape[1]
    out = resid_ref[...]
    for b in range(w_ref.shape[0]):
        pl.when(pl.program_id(0) == 0)(functools.partial(arrive, w_ref.at[b], sem.at[b]))
        stop = min(width, units - b * width)
        out = out + dot_nt(mixed_ref[:, b * width : b * width + stop], w_ref[b, :, :stop])
    out_ref[...] = out.astype(BF16)


def ffn_out(resid, mixed, weights, rows_ff):
    count, width = resid.shape
    units = mixed.shape[1]
    spans = -(-units // width)
    rows = lambda columns: pl.BlockSpec((256, columns), lambda i, *_: (i, 0))
    return fetching_call(
        functools.partial(ffn_out_kernel, rows_ff),
        [weights],
        name="ffn_output",
        grid=(count // 256,),
        in_specs=[rows(width), rows(units)],
        out_specs=[rows(width)],
        out_shape=[sds((count, width), BF16)],
        scratch=[pltpu.VMEM((spans, width, width), BF16), pltpu.SemaphoreType.DMA((spans,))],
        flops=2 * count * width * units,
        nbytes=2 * (count * units + 3 * count * width + units * width),
    )(resid, mixed)[0]


def project_grad_kernel(gp_ref, hid_ref, out_ref):
    out_ref[...] = dot_tn(gp_ref[0], hid_ref[...]).astype(BF16)


def project_grad(grad_projected, hidden):
    count, width = hidden.shape
    block = 512
    per = width // block
    return call(
        project_grad_kernel,
        name="grad_qkv",
        grid=(3 * per,),
        in_specs=[pl.BlockSpec((1, count, block), lambda j: (j // per, 0, j % per)), whole((count, width))],
        out_specs=pl.BlockSpec((block, width), lambda j: (j, 0)),
        out_shape=sds((3 * width, width), BF16),
        flops=6 * count * width * width,
        nbytes=2 * 7 * count * width,
    )(grad_projected, hidden)


def project_grad_halves_kernel(rows, core_ref, gp_ref, hid_ref, stay_ref, go_ref, acc_ref):
    step = pl.program_id(0)
    block, width = acc_ref.shape

    def product(k):
        parts, at = [], k * block
        while at < (k + 1) * block:
            stop = min((k + 1) * block, (at // width + 1) * width)
            parts.append(gp_ref[at // width, :, at % width : at % width + stop - at])
            at = stop
        acc_ref[...] = dot_tn(jnp.concatenate(parts, axis=1), hid_ref[...])

    for k in range(gp_ref.shape[0] * width // block):
        pl.when(step == k)(functools.partial(product, k))
    mine = core_ref[0]
    for pair in range(block // (2 * rows)):
        to = slice(pair * rows, (pair + 1) * rows)
        for out, core in ((stay_ref, mine), (go_ref, 1 - mine)):
            start = pl.multiple_of((2 * pair + core) * rows, rows)
            out[to, :] = acc_ref[pl.ds(start, rows), :].astype(BF16)


def project_grad_halves(grad_projected, hidden, rows, core):
    count, width = hidden.shape
    total = 3 * width
    block = next(b for b in range(LANES, total + 1, LANES) if b % (2 * rows) == 0 and total % b == 0)
    half = pl.BlockSpec((block // 2, width), lambda j, _: (j, 0))
    return pl.pallas_call(
        functools.partial(project_grad_halves_kernel, rows),
        name="grad_qkv",
        grid_spec=pltpu.PrefetchScalarGridSpec(
            num_scalar_prefetch=1,
            grid=(total // block,),
            in_specs=[whole(grad_projected.shape, once=True), whole((count, width))],
            out_specs=[half, half],
            scratch_shapes=[pltpu.VMEM((block, width), F32)],
        ),
        out_shape=[sds((total // 2, width), BF16)] * 2,
        compiler_params=pltpu.CompilerParams(
            dimension_semantics=("arbitrary",), vmem_limit_bytes=VMEM_BYTES
        ),
        cost_estimate=pl.CostEstimate(
            flops=6 * count * width * width, transcendentals=0, bytes_accessed=14 * count * width
        ),
    )(core.reshape(1).astype(jnp.int32), grad_projected, hidden)


def hidden_back_kernel(rows_qkv, group, groups, weights, gp_ref, out_ref, w_ref, sem):
    step = pl.program_id(0)
    block = gp_ref.shape[2]

    @pl.when(step == 0)
    def _():
        fetch(weights, 0, rows_qkv, w_ref, sem, group)

    arrive_in_time(w_ref, sem, group * rows_qkv, range(groups), block, step)
    term = dot_nn(gp_ref[0], w_ref[pl.ds(pl.multiple_of(step * block, block), block), :])

    @pl.when(step == 0)
    def _():
        out_ref[...] = term

    @pl.when(step > 0)
    def _():
        out_ref[...] += term


def hidden_back(grad_projected, weights, rows_qkv):
    _, count, width = grad_projected.shape
    group, groups = grouping(weights, 4)
    return fetching_call(
        functools.partial(hidden_back_kernel, rows_qkv, group, groups),
        [weights],
        name="grad_hidden_one",
        grid=(3,),
        in_specs=[pl.BlockSpec((1, count, width), lambda j, *_: (j, 0, 0))],
        out_specs=[whole((count, width))],
        out_shape=[sds((count, width), F32)],
        scratch=[pltpu.VMEM((3 * width, width), BF16), pltpu.SemaphoreType.DMA((groups,))],
        flops=6 * count * width * width,
        nbytes=2 * 8 * count * width,
    )(grad_projected)[0]


def norm_back_kernel(grad_ref, tok_ref, mid_ref, gain_ref, out_ref, gnorm_ref):
    normed, inverse = normalise(tok_ref[...].astype(F32))
    grad = grad_ref[...]
    part = jnp.sum(grad * normed, axis=0, keepdims=True)
    hat = grad * gain_ref[:1, :]
    first = jnp.mean(hat, axis=-1, keepdims=True)
    second = jnp.mean(hat * normed, axis=-1, keepdims=True)
    out_ref[...] = mid_ref[...] + inverse * (hat - first - normed * second)

    @pl.when(pl.program_id(0) == 0)
    def _():
        gnorm_ref[...] = part

    @pl.when(pl.program_id(0) > 0)
    def _():
        gnorm_ref[...] += part


def norm_back(grad, tokens, mid, gain):
    count, width = tokens.shape
    rows = pl.BlockSpec((128, width), lambda i: (i, 0))
    return call(
        norm_back_kernel,
        name="grad_tokens",
        grid=(count // 128,),
        in_specs=[rows, rows, rows, whole((2, width))],
        out_specs=[rows, whole((1, width))],
        out_shape=[sds((count, width), F32), sds((1, width), F32)],
        flops=20 * count * width,
        nbytes=14 * count * width,
    )(grad, tokens, mid, gain)


Z, Y, X = 4, 2, 2
UP, DOWN, IN_Y, IN_X = (1, 0, 0), (-1, 0, 0), (0, 1, 0), (0, 0, 1)
CROSSED, LEVEL, UPRIGHT = ("planes", "lines"), ("planes", "planes"), ("lines", "lines")
SPREAD = {
    CROSSED: (((UP, IN_X), (DOWN, IN_Y), (UP, IN_Y)), ((IN_Y, UP), (IN_X, DOWN), (IN_X, UP))),
    LEVEL: (((UP, UP), (DOWN, DOWN), (UP, UP)), ((IN_Y, IN_X), (IN_X, IN_Y), (IN_X, IN_Y))),
    UPRIGHT: (((IN_X, IN_Y), (IN_Y, IN_X), (IN_Y, IN_X)), ((UP, UP), (DOWN, DOWN), (UP, UP))),
}
REDUCE = {
    CROSSED: (((IN_X, DOWN), (IN_X, UP), (IN_Y, DOWN)), ((DOWN, IN_Y), (UP, IN_Y), (DOWN, IN_X))),
    LEVEL: (((IN_X, IN_Y), (IN_X, IN_Y), (IN_Y, IN_X)), ((DOWN, DOWN), (UP, UP), (DOWN, DOWN))),
    UPRIGHT: (((DOWN, DOWN), (UP, UP), (DOWN, DOWN)), ((IN_Y, IN_X), (IN_Y, IN_X), (IN_X, IN_Y))),
}


def ident(z, y, x, c):
    return (((z % Z) * Y + y % Y) * X + x % X) * 2 + c


def plus(*moves):
    return tuple(sum(m[i] for m in moves) for i in range(3))


def minus(move):
    return tuple(-m for m in move)


def hop(array, axis, moves):
    pairs = [
        (ident(z, y, x, c), ident(z + m[0], y + m[1], x + m[2], c))
        for z in range(Z) for y in range(Y) for x in range(X)
        for c, m in enumerate(moves)
    ]
    return lax.ppermute(array, axis, pairs)


def swap_cores(array, axis):
    return lax.ppermute(array, axis, [(i, i ^ 1) for i in range(2 * Z * Y * X)])


def place(axis):
    me = lax.axis_index(axis)
    return (me // (2 * Y * X), me // (2 * X) % Y, me // 2 % X), me % 2


def by_core(c, zero, one):
    return jnp.where(c == 0, jnp.stack(zero), jnp.stack(one)).astype(jnp.int32)


def together(*places):
    values = lax.optimization_barrier(tuple(getattr(owner, name) for owner, name in places))
    for (owner, name), value in zip(places, values, strict=True):
        setattr(owner, name, value)


def tie(*values):
    return lax.optimization_barrier(values)


class Spread:
    def __init__(self, shard, axis, route):
        self.shard, self.axis, self.route = shard, axis, route

    def near(self):
        short, _ = SPREAD[self.route]
        self.first = hop(self.shard, self.axis, short[0])
        self.third = hop(self.shard, self.axis, short[1])

    def nearer(self):
        short, _ = SPREAD[self.route]
        second = hop(self.first, self.axis, short[2])
        self.block = jnp.stack([self.shard, self.first, second, self.third])

    def far_one(self):
        self.one = hop(self.block, self.axis, SPREAD[self.route][1][0])

    def far_three(self):
        self.three = hop(self.block, self.axis, SPREAD[self.route][1][1])

    def farther(self):
        _, far = SPREAD[self.route]
        self.two = hop(self.one, self.axis, far[2])

    def swap(self, *names):
        for name in names:
            setattr(self, "other_" + name, swap_cores(getattr(self, name), self.axis))

    def result(self):
        short, far = SPREAD[self.route]
        names = ("block", "one", "two", "three")
        pieces = tuple(getattr(self, kind + name) for kind in ("", "other_") for name in names)
        at, c = place(self.axis)
        froms = []
        for core in range(2):
            s, f = [m[core] for m in short], [m[core] for m in far]
            close = [(0, 0, 0), s[0], plus(s[0], s[2]), s[1]]
            long = [(0, 0, 0), f[0], plus(f[0], f[2]), f[1]]
            froms.append([ident(*plus(at, minus(a), minus(b)), core) for a in long for b in close])
        order = jnp.concatenate([by_core(c, *froms), by_core(c, *froms[::-1])])
        return order, pieces


def lay_out(grad, wide):
    spans = [(b, min(b + wide, grad.shape[2])) for b in range(0, grad.shape[2], wide)]
    return spans, grad.shape[1] * len(spans)


def gather_rows(mine, theirs, more, out, wide):
    at = 0
    for g, t in zip(mine, theirs, strict=True):
        rows = g.shape[1]
        for a, b in lay_out(g, wide)[0]:
            value = g[0, :, a:b].astype(F32) + t[0, :, a:b].astype(F32)
            for m in more:
                value = value + m[at : at + rows, : b - a].astype(F32)
            out[at : at + rows, : b - a] = value.astype(out.dtype)
            if b - a < wide:
                out[at : at + rows, b - a :] = jnp.zeros((rows, wide - (b - a)), out.dtype)
            at += rows


def collect_call(kernel, name, chosen, lines, splits, in_specs, out_specs, out_shape, nbytes, args):
    return pl.pallas_call(
        kernel,
        name=name,
        grid_spec=pltpu.PrefetchScalarGridSpec(
            num_scalar_prefetch=1, grid=(lines, splits), in_specs=in_specs, out_specs=out_specs
        ),
        out_shape=out_shape,
        compiler_params=pltpu.CompilerParams(
            dimension_semantics=("arbitrary", "arbitrary"), vmem_limit_bytes=VMEM_BYTES
        ),
        cost_estimate=pl.CostEstimate(flops=nbytes, transcendentals=0, bytes_accessed=nbytes),
    )(chosen, *args)


def collect(grads, twins, extras, chosen, lines, wide):
    four = chosen.shape[1]
    total = sum(lay_out(g, wide)[1] for g in grads)
    k, number = len(grads) * four, len(lines)
    splits, part = 1, wide

    def kernel(chosen_ref, *refs):
        mine, theirs, more, outs = refs[:k], refs[k : 2 * k], refs[2 * k : -number], refs[-number:]

        def fill(out):
            for i in range(four):
                gather_rows(mine[i::four], theirs[i::four], [m.at[i] for m in more], out.at[i], part)

        for j, out in enumerate(outs):
            pl.when(pl.program_id(0) == j)(functools.partial(fill, out))

    def by_device(g, i):
        def index(j, q, chosen_ref):
            device = chosen_ref[lines[0], i]
            for step, which in enumerate(lines[1:], 1):
                device = jnp.where(j == step, chosen_ref[which, i], device)
            return device, 0, q

        return pl.BlockSpec((1, g.shape[1], g.shape[2] // splits), index)

    def output(step):
        index = lambda j, q, _: (0, 0, jnp.where(j < step, 0, jnp.where(j > step, splits - 1, q)))
        return pl.BlockSpec((four, total, part), index)

    arrived = pl.BlockSpec((four, total, part), lambda j, q, _: (0, 0, q))
    devices = [by_device(g, i) for g in grads for i in range(four)]
    return collect_call(
        kernel,
        "collect_grads",
        chosen,
        number,
        splits,
        devices * 2 + [arrived] * len(extras),
        [output(j) for j in range(number)],
        [sds((four, total, wide), BF16)] * number,
        2 * number * four * total * wide * (3 + len(extras)),
        [*(g for g in (*grads, *twins) for _ in range(four)), *extras],
    )


def collect_last(grads, twins, extras, chosen, wide, direct):
    four = chosen.shape[1]
    total = sum(lay_out(g, wide)[1] for g in grads)
    k = len(grads) * four

    def kernel(chosen_ref, *refs):
        mine, theirs, more, outs = refs[:k], refs[k : 2 * k], refs[2 * k : -four], refs[-four:]
        for i, out in enumerate(outs):
            gather_rows(mine[i::four], theirs[i::four], [m.at[0] for m in more[i::four]], out, wide)

    def pick(shape, line, i):
        return pl.BlockSpec((1, *shape[1:]), lambda j, q, chosen_ref: (chosen_ref[line, i], 0, 0))

    devices = [pick(g.shape, 3, i) for g in grads for i in range(four)]
    places = [pick(m.shape, 4, i) for m in extras for i in range(four)]
    return collect_call(
        kernel,
        "collect_last_grads",
        chosen,
        1,
        1,
        devices * 2 + places,
        [whole((total, wide))] * four,
        [sds((total, wide), kind) for kind in (BF16, BF16, BF16 if direct else F32, F32)],
        2 * four * total * wide * (4 + len(extras)),
        [a for a in (*grads, *twins, *extras) for _ in range(four)],
    )


class Reduce:
    def __init__(self, axis, route, wide, halves=False, direct=False):
        self.axis, self.route, self.wide, self.halves, self.direct = axis, route, wide, halves, direct
        far, short = REDUCE[route]
        at, c = place(axis)
        both = lambda a, b: tuple(plus(i, j) for i, j in zip(a, b, strict=True))
        here = ((0, 0, 0), (0, 0, 0))

        def line(step):
            lists = []
            for core, kind in enumerate(route):
                z, y, x = plus(at, step[core])
                if kind == "planes":
                    lists.append([ident(k, y, x, core) for k in range(Z)])
                else:
                    lists.append([ident(z, j, k, core) for j in range(Y) for k in range(X)])
            return by_core(c, *lists)

        def slot(step):
            places = []
            for core, kind in enumerate(route):
                z, y, x = plus(at, step[core])
                places.append(z % Z if kind == "planes" else y % Y * X + x % X)
            return jnp.where(c == 0, places[0], places[1])

        ends = (both(short[0], short[2]), short[1], short[2], here)
        slots = jnp.stack([slot(step) for step in ends]).astype(jnp.int32)
        lines = [line(step) for step in (both(far[0], far[2]), far[1], far[2])]
        last = []
        for core in range(2):
            last.append([ident(*plus(at, step[core]), core) for step in ends])
        devices = jnp.stack([*lines, by_core(c, *last)])
        self.chosen = jnp.concatenate([devices // 2 if halves else devices, slots[None]])

    def pair(self, grads, go=None):
        self.grads = grads
        self.twins = tuple(swap_cores(g, self.axis) for g in (go if self.halves else grads))

    def pack(self):
        self.one, self.two = collect(self.grads, self.twins, (), self.chosen, (0, 1), self.wide)

    def far(self):
        far, _ = REDUCE[self.route]
        self.one, self.two = hop(self.one, self.axis, far[0]), hop(self.two, self.axis, far[1])

    def repack(self):
        (self.three,) = collect(self.grads, self.twins, (self.one,), self.chosen, (2,), self.wide)

    def farther(self):
        far, _ = REDUCE[self.route]
        self.three = hop(self.three, self.axis, far[2])

    def gather(self):
        self.one, self.two, self.three, self.rest = collect_last(
            self.grads, self.twins, (self.two, self.three), self.chosen, self.wide, self.direct
        )

    def near(self):
        _, short = REDUCE[self.route]
        first = short[0]
        if self.direct:
            first = tuple(plus(a, b) for a, b in zip(short[0], short[2], strict=True))
            self.three = hop(self.three, self.axis, short[2])
        self.one, self.two = hop(self.one, self.axis, first), hop(self.two, self.axis, short[1])

    def nearer(self):
        _, short = REDUCE[self.route]
        self.three = hop((self.three + self.one.astype(F32)).astype(BF16), self.axis, short[2])

    def result(self):
        total = self.rest + self.two.astype(F32) + self.three.astype(F32)
        return total + self.one.astype(F32) if self.direct else total


def tables(segment):
    count = segment.shape[0]
    slots = jnp.arange(count, dtype=jnp.int32)
    order = jnp.where(segment < 0, count, segment)
    starts = jnp.sum((order[None, :] < order[:, None]).astype(jnp.int32), axis=1)
    positions = (slots - starts).astype(F32)
    half = HD // 2
    freqs = THETA ** (-2.0 * jnp.arange(half, dtype=F32) / HD)
    angles = positions[:, None] * freqs[None, :]
    cosine, sine = jnp.cos(angles), jnp.sin(angles)
    cosine = jnp.concatenate([cosine] * 4, axis=1)
    sine = jnp.concatenate([-sine, sine] * 2, axis=1)
    group = jnp.where(segment < 0, -1 - slots, segment)
    return cosine, sine, jnp.broadcast_to(group[:, None], (count, LANES)), group[None, :]


def spans_of(matrix, wide):
    rows, columns = matrix.shape
    count = -(-columns // wide)
    matrix = jnp.pad(matrix, ((0, 0), (0, count * wide - columns)))
    return matrix.reshape(rows, count, wide).transpose(1, 0, 2).reshape(count * rows, wide)


def pad_units(w_ff_out, n, padded):
    units = w_ff_out.reshape(w_ff_out.shape[0], n // 2, -1)
    return jnp.pad(units, ((0, 0), (0, 0), (0, padded - units.shape[2]))).reshape(w_ff_out.shape[0], -1)


def drop_units(g_ff, n, padded, rows_in):
    return g_ff.reshape(-1, n // 2, padded)[:, :, :rows_in].reshape(-1, n // 2 * rows_in)


def sum_norms(n, axis, g_one, g_two):
    g_norms = jnp.stack([g_one.reshape(n, -1), g_two.reshape(n, -1)], axis=1)
    g_norms = jnp.sum(lax.all_to_all(g_norms, axis, 0, 0, tiled=True), axis=0)
    return g_norms


def by_collectives(tokens, cotangent, segment, w_qkv, w_attn_out, w_in, w_ff_out, gains, w_in_rows, padded, axis):
    n = lax.axis_size(axis)
    width = tokens.shape[1]
    units = n // 2 * padded
    pairs = width // LANES
    gather = lambda shard: lax.all_gather(shard, axis, axis=0, tiled=True)
    at_once = lambda matrix: (jnp.zeros((1,), jnp.int32), (matrix[None],))
    w_qkv, w_ff = at_once(gather(w_qkv)), at_once(spans_of(gather(pad_units(w_ff_out, n, padded)), width))
    w_in = at_once(jnp.concatenate([gather(w_in), gather(w_attn_out)]))
    gains = gather(gains.reshape(1, 2, -1)).astype(F32).transpose(1, 0, 2).reshape(2, width)
    cosine, sine, seg_column, seg_row = tables(segment)
    qkv, hidden_one, gains = project(tokens, cosine, sine, w_qkv, 3 * width, gains)
    attn_out, lse = attend(qkv, seg_column, seg_row, width, 0, pairs)
    resid, mixed, mid, grad_heads, g_out, g_two, g_in, g_ff = ffn(
        tokens, attn_out, cotangent, gains, w_in, w_ff, units, 2 * units, width, width
    )
    output = ffn_out(resid, mixed, w_ff, width)
    grad_projected = attend_back(qkv, attn_out, grad_heads, lse, seg_column, seg_row, cosine, sine, 0, pairs)
    g_qkv = project_grad(grad_projected, hidden_one)
    grad_tokens, g_one = norm_back(hidden_back(grad_projected, w_qkv, 3 * width), tokens, mid, gains)
    scatter = lambda grad: lax.psum_scatter(grad, axis, scatter_dimension=0, tiled=True).astype(F32)
    g_in = g_in.reshape(2 * units, width)
    g_ff = drop_units(scatter(g_ff), n, padded, w_in_rows)
    return output, grad_tokens, scatter(g_qkv), scatter(g_out), scatter(g_in), g_ff, g_one, g_two


class Box:
    pass


def by_links(tokens, cotangent, segment, w_qkv, w_attn_out, w_in, w_ff_out, gains, w_in_rows, padded, axis):
    n = lax.axis_size(axis)
    width = tokens.shape[1]
    units = n // 2 * padded
    pairs = width // LANES
    rows_qkv, rows_out, rows_ff = w_qkv.shape[0], w_attn_out.shape[0], w_ff_out.shape[0]
    v = Box()
    gain_rows = jnp.pad(gains[None], ((0, 7), (0, width - gains.shape[0])))
    s_qkv = Spread(jnp.concatenate([w_qkv, gain_rows]), axis, LEVEL)
    s_in = Spread(jnp.concatenate([w_in, w_attn_out]), axis, LEVEL)
    s_ff = Spread(spans_of(pad_units(w_ff_out, n, padded), width), axis, UPRIGHT)
    r_ff = Reduce(axis, UPRIGHT, width, direct=True)
    r_in = Reduce(axis, LEVEL, width)
    r_qkv = Reduce(axis, LEVEL, width, halves=True, direct=True)
    v.cosine, v.sine, v.seg_column, v.seg_row = tables(segment)

    s_qkv.near()
    s_ff.near()
    s_qkv.nearer()
    s_ff.nearer()
    together((s_qkv, "block"), (s_in, "shard"), (s_ff, "block"), *((v, k) for k in vars(v)))
    s_qkv.far_one()
    s_qkv.far_three()
    s_in.near()
    s_qkv.swap("block")
    together((s_qkv, "one"), (s_qkv, "three"), (s_qkv, "other_block"), (s_in, "first"), (s_in, "third"))
    s_qkv.farther()
    s_in.nearer()
    s_qkv.swap("one", "three")
    together((s_qkv, "two"), (s_qkv, "other_three"), (s_qkv, "other_one"), (s_in, "block"), (s_ff, "block"))
    s_in.far_one()
    s_in.far_three()
    s_ff.far_one()
    s_qkv.swap("two")
    s_ff.swap("block")
    w_qkv = s_qkv.result()
    v.qkv, v.hidden_one, v.gains = project(tokens, v.cosine, v.sine, w_qkv, rows_qkv)
    together((v, "qkv"), (s_ff, "one"), (s_ff, "block"), (s_in, "block"), (s_ff, "other_block"))
    s_ff.far_three()
    s_ff.swap("one")
    s_in.swap("block")
    attend_some = lambda first, number, done=None: attend(v.qkv, v.seg_column, v.seg_row, width, first, number, done)
    v.done = attend_some(0, pairs // 2)
    together(
        (v, "done"), (s_in, "one"), (s_in, "three"), (s_ff, "one"), (s_ff, "three"),
        (s_in, "other_block"), (s_ff, "other_one"),
    )
    s_in.farther()
    s_ff.farther()
    s_in.swap("one", "three")
    s_ff.swap("three")
    v.done = attend_some(pairs // 2, pairs // 2, v.done)
    together(
        (v, "done"), (s_in, "two"), (s_ff, "two"), (s_in, "other_one"), (s_in, "other_three"), (s_ff, "other_three")
    )
    s_in.swap("two")
    s_ff.swap("two")
    attn_out, lse = v.done
    w_in, w_ff = s_in.result(), s_ff.result()
    rows_of = lambda grad: grad.reshape(n, -1, grad.shape[-1])
    resid, v.mixed, mid, v.heads, v.g_out, g_two, v.g_in, g_ff = ffn(
        tokens, attn_out, cotangent, v.gains, w_in, w_ff, units, padded, rows_out, rows_ff
    )

    def back(first, number):
        v.some = attend_back(
            v.qkv, attn_out, v.heads, lse, v.seg_column, v.seg_row, v.cosine, v.sine,
            first * pairs // 8, number * pairs // 8, v.some,
        )

    v.some = None
    r_ff.pair((rows_of(g_ff),))
    back(0, 1)
    together((v, "some"), (r_ff, "twins"), (v, "g_in"), (v, "g_out"))
    r_in.pair((rows_of(v.g_in), rows_of(v.g_out)))
    r_ff.pack()
    together((v, "some"), (r_ff, "one"), (r_ff, "two"))
    r_ff.far()
    back(1, 2)
    together((v, "some"), (r_in, "twins"))
    r_in.pack()
    together((v, "some"), (r_in, "one"), (r_in, "two"))
    r_in.far()
    back(3, 2)
    together((v, "some"), (r_ff, "one"), (r_ff, "two"))
    r_ff.repack()
    together((v, "some"), (r_ff, "three"))
    r_ff.farther()
    back(5, 2)
    together((v, "some"), (r_in, "one"), (r_in, "two"), (r_ff, "three"))
    r_in.repack()
    together((v, "some"), (r_in, "three"), (r_ff, "three"))
    r_in.farther()
    back(7, 1)
    together((v, "some"), (r_ff, "three"))
    r_ff.gather()
    together((v, "some"), (r_ff, "one"), (r_ff, "two"))
    r_ff.near()
    v.stay, v.go = project_grad_halves(v.some, v.hidden_one, rows_qkv, place(axis)[1])
    together((v, "some"), (v, "stay"), (v, "go"), (r_in, "three"), (r_ff, "one"), (r_ff, "two"), (r_ff, "three"))
    half_of = lambda grad: grad.reshape(n // 2, -1, width)
    r_qkv.pair((half_of(v.stay),), (half_of(v.go),))
    r_in.gather()
    together((v, "some"), (r_qkv, "twins"), (r_in, "one"), (r_in, "two"))
    r_in.near()
    r_qkv.pack()
    together((v, "some"), (r_qkv, "one"), (r_qkv, "two"))
    r_qkv.far()
    v.hidden = hidden_back(v.some, w_qkv, rows_qkv)
    together((v, "hidden"), (r_ff, "one"), (r_ff, "two"), (r_ff, "three"))
    g_ff = r_ff.result().reshape(-1, rows_ff, width).transpose(1, 0, 2).reshape(rows_ff, -1)[:, :units]
    v.g_ff = drop_units(g_ff, n, padded, w_in_rows)
    together((v, "g_ff"), (v, "hidden"), (r_qkv, "one"), (r_qkv, "two"), (r_in, "one"), (r_in, "two"))
    r_qkv.repack()
    together((v, "hidden"), (r_qkv, "three"))
    r_qkv.farther()
    r_in.nearer()
    v.grad_tokens, v.g_one = norm_back(v.hidden, tokens, mid, v.gains)
    together((v, "grad_tokens"), (v, "g_one"), (r_qkv, "three"), (r_in, "three"))
    r_qkv.gather()
    together((v, "mixed"), (r_qkv, "one"), (r_qkv, "two"), (r_qkv, "three"), (r_qkv, "rest"))
    r_qkv.near()
    v.output = ffn_out(resid, v.mixed, w_ff, rows_ff)
    together((v, "output"), (r_qkv, "one"), (r_qkv, "two"), (r_qkv, "three"), (r_in, "three"))
    rest = r_in.result()
    return v.output, v.grad_tokens, r_qkv.result(), rest[padded:], rest[:padded], v.g_ff, v.g_one, g_two


def body(tokens, cotangent, segment, w_qkv, w_attn_out, w_in, w_ff_out, norm_one, norm_two):
    axis = "fsdp"
    n = lax.axis_size(axis)
    rows_in = w_in.shape[0]
    padded = -(-rows_in // 16) * 16
    w_in = jnp.pad(w_in, ((0, padded - rows_in), (0, 0)))
    scales = norm_one.shape[0]
    aligned = not (any(w.shape[0] % 16 for w in (w_qkv, w_attn_out, w_ff_out)) or scales & (scales - 1))
    way = by_links if aligned and n == 2 * Z * Y * X else by_collectives
    output, grad_tokens, g_qkv, g_out, g_in, g_ff, g_one, g_two = way(
        tokens, cotangent, segment, w_qkv, w_attn_out, w_in, w_ff_out, jnp.concatenate([norm_one, norm_two]), rows_in, padded, axis
    )
    g_norms = sum_norms(n, axis, g_one, g_two)
    g_in = g_in[:rows_in]
    return (output, grad_tokens, g_qkv, g_out, g_in, g_ff, g_norms[0], g_norms[1])


def solution(mesh):
    rows, flat = P("fsdp", None), P("fsdp")
    return jax.shard_map(
        body,
        mesh=mesh,
        in_specs=(rows, rows, flat, rows, rows, rows, rows, flat, flat),
        out_specs=(rows, rows, rows, rows, rows, rows, flat, flat),
        check_vma=False,
    )
```

profile of v0, /device:TPU:0, one launch (start us, length us, event | category | flops | bytes accessed | tf_op | source)
XLA Modules:
  0.0 426.0 jit_solution(12423985669325289182)
XLA Ops:
  21.0 4.6 %collective-permute-done.1 = bf16[104,1024]{1,0:T(8,128)(2,1)S(1)} collective-permute-done((bf16[104,1024]{1,0:T(8,128)(2,1)S(1)}, bf16[104,1024]{1,0:T(8,128)(2,1)S(1)}, u32[]{:S(2)}, u32[]{:S(2)}) %collective-permute-start.1) | collective-permute-done | bytes 213024 | tf_op jit(solution)/shard_map/ppermute | solution.py:688
  29.7 10.5 %collective-permute-done.10 = bf16[208,1024]{1,0:T(8,128)(2,1)S(1)} collective-permute-done((bf16[208,1024]{1,0:T(8,128)(2,1)S(1)}, bf16[208,1024]{1,0:T(8,128)(2,1)S(1)}, u32[]{:S(2)}, u32[]{:S(2)}) %collective-permute-start.10) | collective-permute-done | bytes 426016 | tf_op jit(solution)/shard_map/ppermute | solution.py:688
  40.1 9.0 %collective-permute-done.9 = bf16[208,1024]{1,0:T(8,128)(2,1)S(1)} collective-permute-done((bf16[208,1024]{1,0:T(8,128)(2,1)S(1)}, bf16[208,1024]{1,0:T(8,128)(2,1)S(1)}, u32[]{:S(2)}, u32[]{:S(2)}) %collective-permute-start.9) | collective-permute-done | bytes 426016 | tf_op jit(solution)/shard_map/ppermute | solution.py:688
  52.8 12.0 %collective-permute-done.14 = bf16[208,1024]{1,0:T(8,128)(2,1)S(1)} collective-permute-done((bf16[208,1024]{1,0:T(8,128)(2,1)S(1)}, bf16[208,1024]{1,0:T(8,128)(2,1)S(1)}, u32[]{:S(2)}, u32[]{:S(2)}) %collective-permute-start.14) | collective-permute-done | bytes 426016 | tf_op jit(solution)/shard_map/ppermute | solution.py:688
  70.6 18.2 %norm_project.1 = (bf16[1024,3072]{1,0:T(8,128)(2,1)}, bf16[1024,1024]{1,0:T(8,128)(2,1)}, f32[2,1024]{1,0:T(2,128)}) custom-call(s32[32]{0:T(128)} %pad_add_fusion.3.refs_0_, bf16[4,104,1024]{2,1,0:T(8,128)(2,1)} %copy-done.5, bf16[4,104,1024]{2,1,0:T(8,128)(2,1)} %copy-done.29, bf16[4,104,1024]{2,1,0:T(8,128)(2,1)} %copy-done.32, ...), custom_call_target="tpu_custom_call" | custom-call | flops 6442450944 | bytes 16777216 | tf_op jit(solution)/shard_map/norm_project/pallas_call | solution.py:140
  88.9 3.8 collective-permute-start.20
  92.9 16.3 %attend.2 = (bf16[1024,1024]{1,0:T(8,128)(2,1)}, f32[8,2,1024]{2,1,0:T(2,128)}) custom-call(bf16[1024,3072]{1,0:T(8,128)(2,1)} %get-tuple-element.169.refs_0_.refs_1_.refs_2_, bf16[1024,3072]{1,0:T(8,128)(2,1)} %get-tuple-element.169.refs_0_.refs_1_.refs_2_, bf16[1024,3072]{1,0:T(8,128)(2,1)} %get-tuple-element.169.refs_0_.refs_1_.refs_2_, ...), custom_call_target="tpu_custom_call" | custom-call | flops 8589934592 | bytes 4194304 | tf_op jit(solution)/shard_map/attend/pallas_call | solution.py:254
  112.5 16.3 %attend.3 = (bf16[1024,1024]{1,0:T(8,128)(2,1)}, f32[8,2,1024]{2,1,0:T(2,128)}) custom-call(bf16[1024,3072]{1,0:T(8,128)(2,1)} %get-tuple-element.169.refs_0_.refs_1_.refs_2_, bf16[1024,3072]{1,0:T(8,128)(2,1)} %get-tuple-element.169.refs_0_.refs_1_.refs_2_, ...), custom_call_target="tpu_custom_call", output_to_operand_aliasing={{0}: (5, {}), {1}: (6, {})} | custom-call | flops 8589934592 | bytes 4194304 | tf_op jit(solution)/shard_map/attend/pallas_call | solution.py:254
  128.8 6.0 %collective-permute-done.24.refs_12_.refs_3_ = bf16[4,96,1024]{2,1,0:T(8,128)(2,1)} collective-permute-done((bf16[4,96,1024]{2,1,0:T(8,128)(2,1)}, bf16[4,96,1024]{2,1,0:T(8,128)(2,1)}, u32[]{:S(2)}, u32[]{:S(2)}) %collective-permute-start.24) | collective-permute-done | bytes 786464 | tf_op jit(solution)/shard_map/ppermute | solution.py:688
  136.1 3.4 collective-permute-done.28.refs_16_.refs_7_
  141.6 78.3 %ffn_forward_backward.1 = (f32[1024,1024]{1,0:T(8,128)}, bf16[1024,2816]{1,0:T(8,128)(2,1)}, f32[1024,1024]{1,0:T(8,128)}, bf16[1024,1024]{1,0:T(8,128)(2,1)}, b...) custom-call(s32[32]{0:T(128)} %pad_add_fusion.3.refs_0_, ...), custom_call_target="tpu_custom_call" | custom-call | flops 47244640256 | bytes 55574528 | tf_op jit(solution)/shard_map/ffn_forward_backward/pallas_call | solution.py:140
  220.3 8.6 %attend_back.5.refs_10_ = bf16[3,1024,1024]{2,1,0:T(8,128)(2,1)} custom-call(bf16[1024,3072]{1,0:T(8,128)(2,1)} %get-tuple-element.169.refs_0_.refs_1_.refs_2_, bf16[1024,3072]{1,0:T(8,128)(2,1)} %get-tuple-element.169.refs_0_.refs_1_.refs_2_, bf16[1024,3072]{1,0:T(8,128)(2,1)} %get-tuple-element.169.refs_0_.refs_1_.refs_2_, ...), custom_call_target="tpu_custom_call" | custom-call | flops 5368709120 | bytes 2097152 | tf_op jit(solution)/shard_map/attend_back/pallas_call | solution.py:325
  232.4 4.0 collect_grads.6
  238.4 14.7 %attend_back.6.refs_10_ = bf16[3,1024,1024]{2,1,0:T(8,128)(2,1)} custom-call(bf16[1024,3072]{1,0:T(8,128)(2,1)} %get-tuple-element.169.refs_0_.refs_1_.refs_2_, bf16[1024,3072]{1,0:T(8,128)(2,1)} %get-tuple-element.169.refs_0_.refs_1_.refs_2_, bf16[1024,3072]{1,0:T(8,128)(2,1)} %get-tuple-element.169.refs_0_.refs_1_.refs_2_, ...), custom_call_target="tpu_custom_call", output_to_operand_aliasing={{}: (10, {})} | custom-call | flops 10737418240 | bytes 4194304 | tf_op jit(solution)/shard_map/attend_back/pallas_call | solution.py:325
  253.2 6.0 %collect_grads.7 = (bf16[4,208,1024]{2,1,0:T(8,128)(2,1)}, bf16[4,208,1024]{2,1,0:T(8,128)(2,1)}) custom-call(s32[5,4]{1,0:T(8,128)} %concatenate.152.chosen_ref, bf16[32,176,1024]{2,1,0:T(8,128)(2,1)} %bitcast.142, bf16[32,176,1024]{2,1,0:T(8,128)(2,1)} %bitcast.143, bf16[32,176,1024]{2,1,0:T(8,128)(2,1)} %bitcast.144, bf16[32,176,1024]{2,1,0:T(8,128)(2,1)} %bitcast.145, ...), custom_call_target="tpu_custom_call" | custom-call | flops 10223616 | bytes 10223616 | tf_op jit(solution)/shard_map/collect_grads/pallas_call | solution.py:777
  261.2 14.9 %attend_back.7.refs_10_ = bf16[3,1024,1024]{2,1,0:T(8,128)(2,1)} custom-call(bf16[1024,3072]{1,0:T(8,128)(2,1)} %get-tuple-element.169.refs_0_.refs_1_.refs_2_, bf16[1024,3072]{1,0:T(8,128)(2,1)} %get-tuple-element.169.refs_0_.refs_1_.refs_2_, bf16[1024,3072]{1,0:T(8,128)(2,1)} %get-tuple-element.169.refs_0_.refs_1_.refs_2_, ...), custom_call_target="tpu_custom_call", output_to_operand_aliasing={{}: (10, {})} | custom-call | flops 10737418240 | bytes 4194304 | tf_op jit(solution)/shard_map/attend_back/pallas_call | solution.py:325
  276.1 3.6 collect_grads.8
  279.7 3.8 collective-permute-start.37
  283.5 15.0 %attend_back.8.refs_10_ = bf16[3,1024,1024]{2,1,0:T(8,128)(2,1)} custom-call(bf16[1024,3072]{1,0:T(8,128)(2,1)} %get-tuple-element.169.refs_0_.refs_1_.refs_2_, bf16[1024,3072]{1,0:T(8,128)(2,1)} %get-tuple-element.169.refs_0_.refs_1_.refs_2_, bf16[1024,3072]{1,0:T(8,128)(2,1)} %get-tuple-element.169.refs_0_.refs_1_.refs_2_, ...), custom_call_target="tpu_custom_call", output_to_operand_aliasing={{}: (10, {})} | custom-call | flops 10737418240 | bytes 4194304 | tf_op jit(solution)/shard_map/attend_back/pallas_call | solution.py:325
  300.0 5.0 %collect_grads.9 = bf16[4,208,1024]{2,1,0:T(8,128)(2,1)} custom-call(s32[5,4]{1,0:T(8,128)} %concatenate.152.chosen_ref, bf16[32,176,1024]{2,1,0:T(8,128)(2,1)} %bitcast.146, bf16[32,176,1024]{2,1,0:T(8,128)(2,1)} %bitcast.147, bf16[32,176,1024]{2,1,0:T(8,128)(2,1)} %bitcast.148, bf16[32,176,1024]{2,1,0:T(8,128)(2,1)} %bitcast.149, ...), custom_call_target="tpu_custom_call" | custom-call | flops 6815744 | bytes 6815744 | tf_op jit(solution)/shard_map/collect_grads/pallas_call | solution.py:777
  305.9 8.7 %attend_back.9.gp_ref.refs_9_ = bf16[3,1024,1024]{2,1,0:T(8,128)(2,1)} custom-call(bf16[1024,3072]{1,0:T(8,128)(2,1)} %get-tuple-element.169.refs_0_.refs_1_.refs_2_, bf16[1024,3072]{1,0:T(8,128)(2,1)} %get-tuple-element.169.refs_0_.refs_1_.refs_2_, bf16[1024,3072]{1,0:T(8,128)(2,1)} %get-tuple-element.169.refs_0_.refs_1_.refs_2_, ...), custom_call_target="tpu_custom_call", output_to_operand_aliasing={{}: (10, {})} | custom-call | flops 5368709120 | bytes 2097152 | tf_op jit(solution)/shard_map/attend_back/pallas_call | solution.py:325
  314.6 3.7 collect_last_grads.3
  321.8 13.6 %grad_qkv.1 = (bf16[1536,1024]{1,0:T(8,128)(2,1)}, bf16[1536,1024]{1,0:T(8,128)(2,1)}) custom-call(s32[1]{0:T(128)} %bitcast.123.core_ref, bf16[3,1024,1024]{2,1,0:T(8,128)(2,1)} %attend_back.9.gp_ref.refs_9_, bf16[1024,1024]{1,0:T(8,128)(2,1)} %get-tuple-element.233.hid_ref), custom_call_target="tpu_custom_call" | custom-call | flops 6442450944 | bytes 14680064 | tf_op jit(solution)/shard_map/grad_qkv/pallas_call | solution.py:565
  336.3 5.5 %collect_last_grads.4 = (bf16[208,1024]{1,0:T(8,128)(2,1)}, bf16[208,1024]{1,0:T(8,128)(2,1)}, f32[208,1024]{1,0:T(8,128)}, f32[208,1024]{1,0:T(8,128)}) custom-call(s32[5,4]{1,0:T(8,128)} %concatenate.152.chosen_ref, bf16[32,176,1024]{2,1,0:T(8,128)(2,1)} %bitcast.150, bf16[32,176,1024]{2,1,0:T(8,128)(2,1)} %bitcast.151, bf16[32,176,1024]{2,1,0:T(8,128)(2,1)} %bitcast.152, ...), custom_call_target="tpu_custom_call" | custom-call | flops 10223616 | bytes 10223616 | tf_op jit(solution)/shard_map/collect_last_grads/pallas_call | solution.py:777
  341.8 4.0 collect_grads.10
  347.9 4.3 %collective-permute-start.45 = (bf16[208,1024]{1,0:T(8,128)(2,1)}, bf16[208,1024]{1,0:T(8,128)(2,1)}, u32[]{:S(2)}, u32[]{:S(2)}) collective-permute-start(bf16[208,1024]{1,0:T(8,128)(2,1)} %get-tuple-element.262), channel_id=1, source_target_pairs={{0,24},{1,25},{2,26},{3,27},{4,28},{5,29},{6,30},{7,31},{8,0},{9,1... | collective-permute-start | bytes 1277960 | tf_op jit(solution)/shard_map/ppermute | solution.py:688
  352.1 15.2 %grad_hidden_one.1.grad_ref = f32[1024,1024]{1,0:T(8,128)} custom-call(s32[32]{0:T(128)} %pad_add_fusion.3.refs_0_, bf16[4,104,1024]{2,1,0:T(8,128)(2,1)} %copy-done.5, bf16[4,104,1024]{2,1,0:T(8,128)(2,1)} %copy-done.29, bf16[4,104,1024]{2,1,0:T(8,128)(2,1)} %copy-done.32, bf16[4,104,1024]{2,1,0:T(8,128)(2,1)} %copy-done.30, ...), custom_call_target="tpu_custom_call" | custom-call | flops 6442450944 | bytes 16777216 | tf_op jit(solution)/shard_map/grad_hidden_one/pallas_call | solution.py:140
  372.3 3.6 collect_grads.11
  379.1 3.3 collective-permute-start.48
  383.7 9.6 %grad_tokens.1 = (f32[1024,1024]{1,0:T(8,128)}, f32[1,1024]{1,0:T(1,128)}) custom-call(f32[1024,1024]{1,0:T(8,128)} %grad_hidden_one.1.grad_ref, bf16[1024,1024]{1,0:T(8,128)(2,1)} %tok_ref.1, f32[1024,1024]{1,0:T(8,128)} %get-tuple-element.268.mid_ref, f32[2,1024]{1,0:T(2,128)} %get-tuple-element.193.refs_21_.gain_ref), custom_call_target="tpu_custom_call" | custom-call | flops 20971520 | bytes 14680064 | tf_op jit(solution)/shard_map/grad_tokens/pallas_call | solution.py:643
  398.6 3.8 collect_last_grads.5
  408.9 12.6 %ffn_output.1 = bf16[1024,1024]{1,0:T(8,128)(2,1)} custom-call(s32[32]{0:T(128)} %pad_add_fusion.2.refs_1_.refs_0_, bf16[4,96,1024]{2,1,0:T(8,128)(2,1)} %pad_maximum_fusion.2.refs_10_.refs_1_, bf16[4,96,1024]{2,1,0:T(8,128)(2,1)} %collective-permute-done.16.refs_11_.refs_2_, bf16[4,96,1024]{2,1,0:T(8,128)(2,1)} %collective-permute-done.24.refs_12_.refs_3_, ...), custom_call_target="tpu_custom_call" | custom-call | flops 5905580032 | bytes 17825792 | tf_op jit(solution)/shard_map/ffn_output/pallas_call | solution.py:140
  (227 shorter events, 82.6 us)
Async XLA Ops:
  26.8 22.3 %collective-permute-start.6 = (bf16[4,104,1024]{2,1,0:T(8,128)(2,1)S(1)}, bf16[4,104,1024]{2,1,0:T(8,128)(2,1)S(1)}, u32[]{:S(2)}, u32[]{:S(2)}) collective-permute-start(bf16[4,104,1024]{2,1,0:T(8,128)(2,1)S(1)} %pad_maximum_fusion.1.refs_1_), channel_id=1, source_target_pairs={{0,4},{1,3},{2,6},{3,1},{4,0},{5,7},{6,2},{7,5},{8,12},{9,11},{10,... | collective-permute-start | bytes 2555912 | tf_op jit(solution)/shard_map/ppermute | solution.py:688
  27.3 21.8 %collective-permute-start.7 = (bf16[4,104,1024]{2,1,0:T(8,128)(2,1)S(1)}, bf16[4,104,1024]{2,1,0:T(8,128)(2,1)S(1)}, u32[]{:S(2)}, u32[]{:S(2)}) collective-permute-start(bf16[4,104,1024]{2,1,0:T(8,128)(2,1)S(1)} %pad_maximum_fusion.1.refs_1_), channel_id=1, source_target_pairs={{0,2},{1,5},{2,0},{3,7},{4,6},{5,1},{6,4},{7,3},{8,10},{9,13},{10,... | collective-permute-start | bytes 2555912 | tf_op jit(solution)/shard_map/ppermute | solution.py:688
  27.6 21.5 %collective-permute-start.8 = (bf16[4,104,1024]{2,1,0:T(8,128)(2,1)S(1)}, bf16[4,104,1024]{2,1,0:T(8,128)(2,1)S(1)}, u32[]{:S(2)}, u32[]{:S(2)}) collective-permute-start(bf16[4,104,1024]{2,1,0:T(8,128)(2,1)S(1)} %pad_maximum_fusion.1.refs_1_), channel_id=1, source_target_pairs={{0,1},{1,0},{2,3},{3,2},{4,5},{5,4},{6,7},{7,6},{8,9},{9,8},{10,11... | collective-permute-start | bytes 2555912 | tf_op jit(solution)/shard_map/ppermute | solution.py:692
  29.5 19.6 %collective-permute-start.9 = (bf16[208,1024]{1,0:T(8,128)(2,1)S(1)}, bf16[208,1024]{1,0:T(8,128)(2,1)S(1)}, u32[]{:S(2)}, u32[]{:S(2)}) collective-permute-start(bf16[208,1024]{1,0:T(8,128)(2,1)S(1)} %fusion.1), channel_id=1, source_target_pairs={{0,8},{1,9},{2,10},{3,11},{4,12},{5,13},{6,14},{7,15},{8,16},{9,17... | collective-permute-start | bytes 1277960 | tf_op jit(solution)/shard_map/ppermute | solution.py:688
  67.4 21.4 %collective-permute-start.16 = (bf16[4,96,1024]{2,1,0:T(8,128)(2,1)}, bf16[4,96,1024]{2,1,0:T(8,128)(2,1)}, u32[]{:S(2)}, u32[]{:S(2)}) collective-permute-start(bf16[4,96,1024]{2,1,0:T(8,128)(2,1)} %pad_maximum_fusion.2.refs_10_.refs_1_), channel_id=1, source_target_pairs={{0,8},{1,9},{2,10},{3,11},{4,12},{5,13},{6,14},{7,15},{8,16},{9,17... | collective-permute-start | bytes 2359304 | tf_op jit(solution)/shard_map/ppermute | solution.py:688
  67.7 21.1 %collective-permute-start.17 = (bf16[4,96,1024]{2,1,0:T(8,128)(2,1)}, bf16[4,96,1024]{2,1,0:T(8,128)(2,1)}, u32[]{:S(2)}, u32[]{:S(2)}) collective-permute-start(bf16[4,96,1024]{2,1,0:T(8,128)(2,1)} %pad_maximum_fusion.2.refs_10_.refs_1_), channel_id=1, source_target_pairs={{0,1},{1,0},{2,3},{3,2},{4,5},{5,4},{6,7},{7,6},{8,9},{9,8},{10,11... | collective-permute-start | bytes 2359304 | tf_op jit(solution)/shard_map/ppermute | solution.py:692
  68.5 41.9 %collective-permute-start.18 = (bf16[4,208,1024]{2,1,0:T(8,128)(2,1)S(1)}, bf16[4,208,1024]{2,1,0:T(8,128)(2,1)}, u32[]{:S(2)}, u32[]{:S(2)}) collective-permute-start(bf16[4,208,1024]{2,1,0:T(8,128)(2,1)S(1)} %pad_maximum_fusion.refs_2_), channel_id=1, source_target_pairs={{0,4},{1,3},{2,6},{3,1},{4,0},{5,7},{6,2},{7,5},{8,12},{9,11},{10,... | collective-permute-start | bytes 5111816 | tf_op jit(solution)/shard_map/ppermute | solution.py:688
  70.0 40.4 %collective-permute-start.19 = (bf16[4,208,1024]{2,1,0:T(8,128)(2,1)S(1)}, bf16[4,208,1024]{2,1,0:T(8,128)(2,1)}, u32[]{:S(2)}, u32[]{:S(2)}) collective-permute-start(bf16[4,208,1024]{2,1,0:T(8,128)(2,1)S(1)} %pad_maximum_fusion.refs_2_), channel_id=1, source_target_pairs={{0,2},{1,5},{2,0},{3,7},{4,6},{5,1},{6,4},{7,3},{8,10},{9,13},{10,... | collective-permute-start | bytes 5111816 | tf_op jit(solution)/shard_map/ppermute | solution.py:688
  88.8 21.6 %collective-permute-start.21 = (bf16[4,208,1024]{2,1,0:T(8,128)(2,1)S(1)}, bf16[4,208,1024]{2,1,0:T(8,128)(2,1)}, u32[]{:S(2)}, u32[]{:S(2)}) collective-permute-start(bf16[4,208,1024]{2,1,0:T(8,128)(2,1)S(1)} %pad_maximum_fusion.refs_2_), channel_id=1, source_target_pairs={{0,1},{1,0},{2,3},{3,2},{4,5},{5,4},{6,7},{7,6},{8,9},{9,8},{10,11... | collective-permute-start | bytes 5111816 | tf_op jit(solution)/shard_map/ppermute | solution.py:692
  88.9 21.5 %collective-permute-start.20 = (bf16[4,96,1024]{2,1,0:T(8,128)(2,1)}, bf16[4,96,1024]{2,1,0:T(8,128)(2,1)}, u32[]{:S(2)}, u32[]{:S(2)}) collective-permute-start(bf16[4,96,1024]{2,1,0:T(8,128)(2,1)} %pad_maximum_fusion.2.refs_10_.refs_1_), channel_id=1, source_target_pairs={{0,24},{1,25},{2,26},{3,27},{4,28},{5,29},{6,30},{7,31},{8,0},{9,1... | collective-permute-start | bytes 2359304 | tf_op jit(solution)/shard_map/ppermute | solution.py:688
  92.7 17.7 %collective-permute-start.22 = (bf16[4,96,1024]{2,1,0:T(8,128)(2,1)}, bf16[4,96,1024]{2,1,0:T(8,128)(2,1)}, u32[]{:S(2)}, u32[]{:S(2)}) collective-permute-start(bf16[4,96,1024]{2,1,0:T(8,128)(2,1)} %collective-permute-done.16.refs_11_.refs_2_), channel_id=1, source_target_pairs={{0,1},{1,0},{2,3},{3,2},{4,5},{5,4},{6,7},{7,6},{8,9},{9,8},{10,11... | collective-permute-start | bytes 2359304 | tf_op jit(solution)/shard_map/ppermute | solution.py:692
  110.4 24.4 %collective-permute-start.23 = (bf16[4,208,1024]{2,1,0:T(8,128)(2,1)}, bf16[4,208,1024]{2,1,0:T(8,128)(2,1)S(1)}, u32[]{:S(2)}, u32[]{:S(2)}) collective-permute-start(bf16[4,208,1024]{2,1,0:T(8,128)(2,1)} %collective-permute-done.18.refs_3_), channel_id=1, source_target_pairs={{0,2},{1,5},{2,0},{3,7},{4,6},{5,1},{6,4},{7,3},{8,10},{9,13},{10,... | collective-permute-start | bytes 5111816 | tf_op jit(solution)/shard_map/ppermute | solution.py:688
  112.0 22.8 %collective-permute-start.25 = (bf16[4,208,1024]{2,1,0:T(8,128)(2,1)}, bf16[4,208,1024]{2,1,0:T(8,128)(2,1)}, u32[]{:S(2)}, u32[]{:S(2)}) collective-permute-start(bf16[4,208,1024]{2,1,0:T(8,128)(2,1)} %collective-permute-done.18.refs_3_), channel_id=1, source_target_pairs={{0,1},{1,0},{2,3},{3,2},{4,5},{5,4},{6,7},{7,6},{8,9},{9,8},{10,11... | collective-permute-start | bytes 5111816 | tf_op jit(solution)/shard_map/ppermute | solution.py:692
  112.0 22.8 %collective-permute-start.26 = (bf16[4,208,1024]{2,1,0:T(8,128)(2,1)}, bf16[4,208,1024]{2,1,0:T(8,128)(2,1)}, u32[]{:S(2)}, u32[]{:S(2)}) collective-permute-start(bf16[4,208,1024]{2,1,0:T(8,128)(2,1)} %collective-permute-done.19.refs_5_), channel_id=1, source_target_pairs={{0,1},{1,0},{2,3},{3,2},{4,5},{5,4},{6,7},{7,6},{8,9},{9,8},{10,11... | collective-permute-start | bytes 5111816 | tf_op jit(solution)/shard_map/ppermute | solution.py:692
  112.5 22.3 %collective-permute-start.24 = (bf16[4,96,1024]{2,1,0:T(8,128)(2,1)}, bf16[4,96,1024]{2,1,0:T(8,128)(2,1)}, u32[]{:S(2)}, u32[]{:S(2)}) collective-permute-start(bf16[4,96,1024]{2,1,0:T(8,128)(2,1)} %collective-permute-done.16.refs_11_.refs_2_), channel_id=1, source_target_pairs={{0,8},{1,9},{2,10},{3,11},{4,12},{5,13},{6,14},{7,15},{8,16},{9,17... | collective-permute-start | bytes 2359304 | tf_op jit(solution)/shard_map/ppermute | solution.py:688
  112.5 22.3 %collective-permute-start.27 = (bf16[4,96,1024]{2,1,0:T(8,128)(2,1)}, bf16[4,96,1024]{2,1,0:T(8,128)(2,1)}, u32[]{:S(2)}, u32[]{:S(2)}) collective-permute-start(bf16[4,96,1024]{2,1,0:T(8,128)(2,1)} %collective-permute-done.20.refs_13_.refs_4_), channel_id=1, source_target_pairs={{0,1},{1,0},{2,3},{3,2},{4,5},{5,4},{6,7},{7,6},{8,9},{9,8},{10,11... | collective-permute-start | bytes 2359304 | tf_op jit(solution)/shard_map/ppermute | solution.py:692
  229.7 23.5 %collective-permute-start.31 = (bf16[32,176,1024]{2,1,0:T(8,128)(2,1)}, bf16[32,176,1024]{2,1,0:T(8,128)(2,1)}, u32[]{:S(2)}, u32[]{:S(2)}) collective-permute-start(bf16[32,176,1024]{2,1,0:T(8,128)(2,1)} %bitcast.141), channel_id=1, source_target_pairs={{0,1},{1,0},{2,3},{3,2},{4,5},{5,4},{6,7},{7,6},{8,9},{9,8},{10,11... | collective-permute-start | bytes 34603016 | tf_op jit(solution)/shard_map/ppermute | solution.py:692
  230.0 23.1 %collective-permute-start.32 = (bf16[32,32,1024]{2,1,0:T(8,128)(2,1)}, bf16[32,32,1024]{2,1,0:T(8,128)(2,1)}, u32[]{:S(2)}, u32[]{:S(2)}) collective-permute-start(bf16[32,32,1024]{2,1,0:T(8,128)(2,1)} %bitcast.179), channel_id=1, source_target_pairs={{0,1},{1,0},{2,3},{3,2},{4,5},{5,4},{6,7},{7,6},{8,9},{9,8},{10,11... | collective-permute-start | bytes 6291464 | tf_op jit(solution)/shard_map/ppermute | solution.py:692
  236.4 39.7 %collective-permute-start.33 = (bf16[4,96,1024]{2,1,0:T(8,128)(2,1)}, bf16[4,96,1024]{2,1,0:T(8,128)(2,1)}, u32[]{:S(2)}, u32[]{:S(2)}) collective-permute-start(bf16[4,96,1024]{2,1,0:T(8,128)(2,1)} %get-tuple-element.214), channel_id=1, source_target_pairs={{0,24},{1,25},{2,26},{3,27},{4,28},{5,29},{6,30},{7,31},{8,0},{9,1... | collective-permute-start | bytes 2359304 | tf_op jit(solution)/shard_map/ppermute | solution.py:688
  238.4 37.7 %collective-permute-start.34 = (bf16[4,96,1024]{2,1,0:T(8,128)(2,1)}, bf16[4,96,1024]{2,1,0:T(8,128)(2,1)}, u32[]{:S(2)}, u32[]{:S(2)}) collective-permute-start(bf16[4,96,1024]{2,1,0:T(8,128)(2,1)} %get-tuple-element.215), channel_id=1, source_target_pairs={{0,8},{1,9},{2,10},{3,11},{4,12},{5,13},{6,14},{7,15},{8,16},{9,17... | collective-permute-start | bytes 2359304 | tf_op jit(solution)/shard_map/ppermute | solution.py:688
  259.1 40.9 %collective-permute-start.35 = (bf16[4,208,1024]{2,1,0:T(8,128)(2,1)}, bf16[4,208,1024]{2,1,0:T(8,128)(2,1)}, u32[]{:S(2)}, u32[]{:S(2)}) collective-permute-start(bf16[4,208,1024]{2,1,0:T(8,128)(2,1)} %get-tuple-element.219), channel_id=1, source_target_pairs={{0,2},{1,5},{2,0},{3,7},{4,6},{5,1},{6,4},{7,3},{8,10},{9,13},{10,... | collective-permute-start | bytes 5111816 | tf_op jit(solution)/shard_map/ppermute | solution.py:688
  260.7 39.3 %collective-permute-start.36 = (bf16[4,208,1024]{2,1,0:T(8,128)(2,1)}, bf16[4,208,1024]{2,1,0:T(8,128)(2,1)S(1)}, u32[]{:S(2)}, u32[]{:S(2)}) collective-permute-start(bf16[4,208,1024]{2,1,0:T(8,128)(2,1)} %get-tuple-element.220), channel_id=1, source_target_pairs={{0,2},{1,5},{2,0},{3,7},{4,6},{5,1},{6,4},{7,3},{8,10},{9,13},{10,... | collective-permute-start | bytes 5111816 | tf_op jit(solution)/shard_map/ppermute | solution.py:688
  279.7 20.3 %collective-permute-start.37 = (bf16[4,96,1024]{2,1,0:T(8,128)(2,1)}, bf16[4,96,1024]{2,1,0:T(8,128)(2,1)}, u32[]{:S(2)}, u32[]{:S(2)}) collective-permute-start(bf16[4,96,1024]{2,1,0:T(8,128)(2,1)} %collect_grads.8), channel_id=1, source_target_pairs={{0,24},{1,25},{2,26},{3,27},{4,28},{5,29},{6,30},{7,31},{8,0},{9,1... | collective-permute-start | bytes 2359304 | tf_op jit(solution)/shard_map/ppermute | solution.py:688
  305.1 30.5 %collective-permute-start.38 = (bf16[4,208,1024]{2,1,0:T(8,128)(2,1)}, bf16[4,208,1024]{2,1,0:T(8,128)(2,1)}, u32[]{:S(2)}, u32[]{:S(2)}) collective-permute-start(bf16[4,208,1024]{2,1,0:T(8,128)(2,1)} %collect_grads.9), channel_id=1, source_target_pairs={{0,4},{1,3},{2,6},{3,1},{4,0},{5,7},{6,2},{7,5},{8,12},{9,11},{10,... | collective-permute-start | bytes 5111816 | tf_op jit(solution)/shard_map/ppermute | solution.py:688
  318.3 17.1 %collective-permute-start.39 = (bf16[96,1024]{1,0:T(8,128)(2,1)}, bf16[96,1024]{1,0:T(8,128)(2,1)S(1)}, u32[]{:S(2)}, u32[]{:S(2)}) collective-permute-start(bf16[96,1024]{1,0:T(8,128)(2,1)} %get-tuple-element.237), channel_id=1, source_target_pairs={{0,6},{1,7},{2,4},{3,5},{4,2},{5,3},{6,0},{7,1},{8,14},{9,15},{10,... | collective-permute-start | bytes 589832 | tf_op jit(solution)/shard_map/ppermute | solution.py:688
  345.8 25.5 %collective-permute-start.43 = (bf16[4,96,1024]{2,1,0:T(8,128)(2,1)}, bf16[4,96,1024]{2,1,0:T(8,128)(2,1)S(1)}, u32[]{:S(2)}, u32[]{:S(2)}) collective-permute-start(bf16[4,96,1024]{2,1,0:T(8,128)(2,1)} %get-tuple-element.260), channel_id=1, source_target_pairs={{0,2},{1,5},{2,0},{3,7},{4,6},{5,1},{6,4},{7,3},{8,10},{9,13},{10,... | collective-permute-start | bytes 2359304 | tf_op jit(solution)/shard_map/ppermute | solution.py:688
  347.3 24.1 %collective-permute-start.44 = (bf16[4,96,1024]{2,1,0:T(8,128)(2,1)}, bf16[4,96,1024]{2,1,0:T(8,128)(2,1)S(1)}, u32[]{:S(2)}, u32[]{:S(2)}) collective-permute-start(bf16[4,96,1024]{2,1,0:T(8,128)(2,1)} %get-tuple-element.261), channel_id=1, source_target_pairs={{0,2},{1,5},{2,0},{3,7},{4,6},{5,1},{6,4},{7,3},{8,10},{9,13},{10,... | collective-permute-start | bytes 2359304 | tf_op jit(solution)/shard_map/ppermute | solution.py:688
  347.9 22.8 %collective-permute-start.45 = (bf16[208,1024]{1,0:T(8,128)(2,1)}, bf16[208,1024]{1,0:T(8,128)(2,1)}, u32[]{:S(2)}, u32[]{:S(2)}) collective-permute-start(bf16[208,1024]{1,0:T(8,128)(2,1)} %get-tuple-element.262), channel_id=1, source_target_pairs={{0,24},{1,25},{2,26},{3,27},{4,28},{5,29},{6,30},{7,31},{8,0},{9,1... | collective-permute-start | bytes 1277960 | tf_op jit(solution)/shard_map/ppermute | solution.py:688
  352.1 19.2 %collective-permute-start.46 = (bf16[208,1024]{1,0:T(8,128)(2,1)}, bf16[208,1024]{1,0:T(8,128)(2,1)S(1)}, u32[]{:S(2)}, u32[]{:S(2)}) collective-permute-start(bf16[208,1024]{1,0:T(8,128)(2,1)} %get-tuple-element.263), channel_id=1, source_target_pairs={{0,8},{1,9},{2,10},{3,11},{4,12},{5,13},{6,14},{7,15},{8,16},{9,17... | collective-permute-start | bytes 1277960 | tf_op jit(solution)/shard_map/ppermute | solution.py:688
  375.9 17.4 %collective-permute-start.47 = (bf16[4,96,1024]{2,1,0:T(8,128)(2,1)}, bf16[4,96,1024]{2,1,0:T(8,128)(2,1)S(1)}, u32[]{:S(2)}, u32[]{:S(2)}) collective-permute-start(bf16[4,96,1024]{2,1,0:T(8,128)(2,1)} %collect_grads.11), channel_id=1, source_target_pairs={{0,4},{1,3},{2,6},{3,1},{4,0},{5,7},{6,2},{7,5},{8,12},{9,11},{10,... | collective-permute-start | bytes 2359304 | tf_op jit(solution)/shard_map/ppermute | solution.py:688
  395.4 26.2 %all-to-all-start = ((f32[32,2,32]{2,1,0:T(2,128)}), f32[32,2,32]{2,1,0:T(2,128)S(1)}, u32[]{:S(2)}, u32[]{:S(2)}) async-start(f32[32,2,32]{2,1,0:T(2,128)} %pad_maximum_fusion.5), calls=%async_computation | async-start | bytes 65536 | tf_op jit(solution)/shard_map/all_to_all | solution.py:973
  402.4 19.7 %collective-permute-start.49 = (bf16[96,1024]{1,0:T(8,128)(2,1)}, bf16[96,1024]{1,0:T(8,128)(2,1)S(1)}, u32[]{:S(2)}, u32[]{:S(2)}) collective-permute-start(bf16[96,1024]{1,0:T(8,128)(2,1)} %get-tuple-element.280), channel_id=1, source_target_pairs={{0,16},{1,17},{2,18},{3,19},{4,20},{5,21},{6,22},{7,23},{8,24},{9,... | collective-permute-start | bytes 589832 | tf_op jit(solution)/shard_map/ppermute | solution.py:688
  (59 other events, 549.9 us)
where the time goes:
time: 433 us; the launch traced here: 426 us
  Pallas kernels  281 us (65%)
  starting transfers between devices  58.2 us (13%)
  waiting for transfers between devices  53.4 us (12%)
  other arithmetic  16.4 us (4%)
  local copies, waits for them, and re-layouts  15.2 us (4%)
    pallas_call x4, Pallas kernels, fetching_call(): return lambda *args: made(*[order for order, _ in weights], *pieces, *args)  124 us
    pallas_call x5, Pallas kernels, attend_back(): call(kernel, name='attend_back', grid=(number,), in_specs=[tall(0), tall(...  61.8 us
    ppermute x36, starting transfers between devices, hop(): return lax.ppermute(array, axis, pairs)  52.1 us
    ppermute x36, waiting for transfers between devices, hop(): return lax.ppermute(array, axis, pairs)  49 us
    pallas_call x9, Pallas kernels, collect_call(): pl.pallas_call(kernel, name=name, grid_spec=pltpu.PrefetchScalarGridSpec(...  39.2 us
    pallas_call x2, Pallas kernels, attend(): call(kernel, name='attend', grid=(number,), in_specs=[tall(0), tall(pairs...  32.6 us
    pallas_call x1, Pallas kernels, project_grad_halves(): pl.pallas_call(functools.partial(project_grad_halves_kernel, rows), name=...  13.6 us
    pallas_call x1, Pallas kernels, norm_back(): call(norm_back_kernel, name='grad_tokens', grid=(count // 128,), in_specs...  9.6 us
  transfers between devices with their start and end apart: 53, of which 14 were waited for; matrix products, arithmetic and copies ran while one was open for 4% of the time, Pallas kernels for 45%

commit v1 on v0

--- a/solution.py
+++ b/solution.py
@@ -77,7 +77,7 @@
     )
 
 
-def fetch(weights, at, rows, target, sem, group=None):
+def fetch(weights, at, rows, target, sem, group=None, columns=slice(None)):
     order_ref, pieces = weights
     i = 0
     for piece in pieces:
@@ -85,8 +85,8 @@
             device = order_ref[i]
             start = pl.multiple_of(device * rows, rows)
             pltpu.make_async_copy(
-                piece.at[slot, pl.ds(at, rows), :],
-                target.at[pl.ds(start, rows), :],
+                piece.at[slot, pl.ds(at, rows), columns],
+                target.at[pl.ds(start, rows), columns],
                 sem if group is None else sem.at[device // group],
             ).start()
             i += 1
@@ -94,6 +94,10 @@
 
 def arrive(target, sem):
     pltpu.make_async_copy(target, target, sem).wait()
+
+
+def spans_of(columns, wide):
+    return [slice(a, min(a + wide, columns)) for a in range(0, columns, wide)]
 
 
 def grouping(weights, group):
@@ -202,7 +206,7 @@
 def project(tokens, cosine, sine, weights, rows, gains=None):
     count, width = tokens.shape
     total = 3 * width
-    block = 512
+    block = width
     given = gains is not None
     group, groups = grouping(weights, 4)
     own = [] if given else [pltpu.VMEM((weights[0].shape[0] * 8, width), BF16), pltpu.SemaphoreType.DMA]
@@ -366,15 +370,16 @@
     block = g_out_ref.shape[1]
     units = w_in_ref.shape[0] // 2
     width = hid_ref.shape[1]
+    spans = spans_of(w_ff_ref.shape[1], width)
     some = 256
 
     @pl.when(step == 0)
     def _():
         fetch(weights_in, rows_in, rows_out, w_attn_ref, sem_attn)
-        fetch(weights_ff, 0, rows_ff, w_ff_ref.at[0], sem_ff.at[0])
+        fetch(weights_ff, 0, rows_ff, w_ff_ref, sem_ff.at[0], columns=spans[0])
         fetch(weights_in, 0, rows_in, w_in_ref, sem_in, group)
-        for b in range(1, w_ff_ref.shape[0]):
-            fetch(weights_ff, b * rows_ff, rows_ff, w_ff_ref.at[b], sem_ff.at[b])
+        for b, span in enumerate(spans[1:], 1):
+            fetch(weights_ff, 0, rows_ff, w_ff_ref, sem_ff.at[b], columns=span)
         cot_t_ref[...] = cot_ref[...].T
         mid_ref[...] = jnp.zeros_like(mid_ref)
         arrive(w_attn_ref, sem_attn)
@@ -389,13 +394,12 @@
     for some_groups in (range(half), range(half, groups)):
         if some_groups:
             arrive_in_time(w_in_ref, sem_in, group * rows_in, some_groups, block, step)
-    for b in range(w_ff_ref.shape[0]):
-        pl.when(step == b * width // block)(functools.partial(arrive, w_ff_ref.at[b], sem_ff.at[b]))
+    for b, span in enumerate(spans):
+        pl.when(step == span.start // block)(functools.partial(arrive, w_ff_ref.at[:, span], sem_ff.at[b]))
     hidden = hid_ref[...]
     w_pre = w_in_ref[pl.ds(pl.multiple_of(step * block, block), block), :]
     w_gate = w_in_ref[pl.ds(pl.multiple_of(units + step * block, block), block), :]
-    per = width // block
-    w_out = w_ff_ref[step // per, :, pl.ds(pl.multiple_of(step % per * block, block), block)]
+    w_out = w_ff_ref[:, pl.ds(pl.multiple_of(step * block, block), block)]
     pre = dot_nt(hidden, w_pre)
     gate = dot_nt(hidden, w_gate)
     grad_mixed = dot_nn(cot_ref[...], w_out)
@@ -437,7 +441,6 @@
 def ffn(tokens, attn_out, cotangent, gains, w_in, w_ff, units, rows_in, rows_out, rows_ff):
     count, width = tokens.shape
     block = 256
-    spans = -(-units // width)
     group, groups = grouping(w_in, 2)
     once = whole((count, width), once=True)
     return fetching_call(
@@ -471,10 +474,10 @@
             pltpu.VMEM((width, count), BF16),
             pltpu.VMEM((width, width), BF16),
             pltpu.VMEM((2 * units, width), BF16),
-            pltpu.VMEM((spans, width, width), BF16),
+            pltpu.VMEM((width, units), BF16),
             pltpu.SemaphoreType.DMA,
             pltpu.SemaphoreType.DMA((groups,)),
-            pltpu.SemaphoreType.DMA((spans,)),
+            pltpu.SemaphoreType.DMA((len(spans_of(units, width)),)),
         ],
         flops=16 * count * width * units,
         nbytes=2 * (10 * count * width + 6 * units * width),
@@ -482,24 +485,23 @@
 
 
 def ffn_out_kernel(rows_ff, weights, resid_ref, mixed_ref, out_ref, w_ref, sem):
+    spans = spans_of(mixed_ref.shape[1], out_ref.shape[1])
+
     @pl.when(pl.program_id(0) == 0)
     def _():
-        for b in range(w_ref.shape[0]):
-            fetch(weights, b * rows_ff, rows_ff, w_ref.at[b], sem.at[b])
-
-    units, width = mixed_ref.shape[1], out_ref.shape[1]
+        for b, span in enumerate(spans):
+            fetch(weights, 0, rows_ff, w_ref, sem.at[b], columns=span)
+
     out = resid_ref[...]
-    for b in range(w_ref.shape[0]):
-        pl.when(pl.program_id(0) == 0)(functools.partial(arrive, w_ref.at[b], sem.at[b]))
-        stop = min(width, units - b * width)
-        out = out + dot_nt(mixed_ref[:, b * width : b * width + stop], w_ref[b, :, :stop])
+    for b, span in enumerate(spans):
+        pl.when(pl.program_id(0) == 0)(functools.partial(arrive, w_ref.at[:, span], sem.at[b]))
+        out = out + dot_nt(mixed_ref[:, span], w_ref[:, span])
     out_ref[...] = out.astype(BF16)
 
 
 def ffn_out(resid, mixed, weights, rows_ff):
     count, width = resid.shape
     units = mixed.shape[1]
-    spans = -(-units // width)
     rows = lambda columns: pl.BlockSpec((256, columns), lambda i, *_: (i, 0))
     return fetching_call(
         functools.partial(ffn_out_kernel, rows_ff),
@@ -509,7 +511,7 @@
         in_specs=[rows(width), rows(units)],
         out_specs=[rows(width)],
         out_shape=[sds((count, width), BF16)],
-        scratch=[pltpu.VMEM((spans, width, width), BF16), pltpu.SemaphoreType.DMA((spans,))],
+        scratch=[pltpu.VMEM((width, units), BF16), pltpu.SemaphoreType.DMA((len(spans_of(units, width)),))],
         flops=2 * count * width * units,
         nbytes=2 * (count * units + 3 * count * width + units * width),
     )(resid, mixed)[0]
@@ -639,11 +641,11 @@
 
 def norm_back(grad, tokens, mid, gain):
     count, width = tokens.shape
-    rows = pl.BlockSpec((128, width), lambda i: (i, 0))
+    rows = pl.BlockSpec((256, width), lambda i: (i, 0))
     return call(
         norm_back_kernel,
         name="grad_tokens",
-        grid=(count // 128,),
+        grid=(count // 256,),
         in_specs=[rows, rows, rows, whole((2, width))],
         out_specs=[rows, whole((1, width))],
         out_shape=[sds((count, width), F32), sds((1, width), F32)],
@@ -952,13 +954,6 @@
     return cosine, sine, jnp.broadcast_to(group[:, None], (count, LANES)), group[None, :]
 
 
-def spans_of(matrix, wide):
-    rows, columns = matrix.shape
-    count = -(-columns // wide)
-    matrix = jnp.pad(matrix, ((0, 0), (0, count * wide - columns)))
-    return matrix.reshape(rows, count, wide).transpose(1, 0, 2).reshape(count * rows, wide)
-
-
 def pad_units(w_ff_out, n, padded):
     units = w_ff_out.reshape(w_ff_out.shape[0], n // 2, -1)
     return jnp.pad(units, ((0, 0), (0, 0), (0, padded - units.shape[2]))).reshape(w_ff_out.shape[0], -1)
@@ -981,7 +976,7 @@
     pairs = width // LANES
     gather = lambda shard: lax.all_gather(shard, axis, axis=0, tiled=True)
     at_once = lambda matrix: (jnp.zeros((1,), jnp.int32), (matrix[None],))
-    w_qkv, w_ff = at_once(gather(w_qkv)), at_once(spans_of(gather(pad_units(w_ff_out, n, padded)), width))
+    w_qkv, w_ff = at_once(gather(w_qkv)), at_once(gather(pad_units(w_ff_out, n, padded)))
     w_in = at_once(jnp.concatenate([gather(w_in), gather(w_attn_out)]))
     gains = gather(gains.reshape(1, 2, -1)).astype(F32).transpose(1, 0, 2).reshape(2, width)
     cosine, sine, seg_column, seg_row = tables(segment)
@@ -1014,8 +1009,9 @@
     gain_rows = jnp.pad(gains[None], ((0, 7), (0, width - gains.shape[0])))
     s_qkv = Spread(jnp.concatenate([w_qkv, gain_rows]), axis, LEVEL)
     s_in = Spread(jnp.concatenate([w_in, w_attn_out]), axis, LEVEL)
-    s_ff = Spread(spans_of(pad_units(w_ff_out, n, padded), width), axis, UPRIGHT)
-    r_ff = Reduce(axis, UPRIGHT, width, direct=True)
+    s_qkv.shard, w_ff_out = tie(s_qkv.shard, w_ff_out)
+    s_ff = Spread(pad_units(w_ff_out, n, padded), axis, UPRIGHT)
+    r_ff = Reduce(axis, UPRIGHT, units, direct=True)
     r_in = Reduce(axis, LEVEL, width)
     r_qkv = Reduce(axis, LEVEL, width, halves=True, direct=True)
     v.cosine, v.sine, v.seg_column, v.seg_row = tables(segment)
@@ -1023,17 +1019,19 @@
     s_qkv.near()
     s_ff.near()
     s_qkv.nearer()
-    s_ff.nearer()
-    together((s_qkv, "block"), (s_in, "shard"), (s_ff, "block"), *((v, k) for k in vars(v)))
+    together((s_qkv, "block"), (s_in, "shard"), (s_ff, "first"), (s_ff, "third"), *((v, k) for k in vars(v)))
     s_qkv.far_one()
     s_qkv.far_three()
     s_in.near()
-    s_qkv.swap("block")
-    together((s_qkv, "one"), (s_qkv, "three"), (s_qkv, "other_block"), (s_in, "first"), (s_in, "third"))
+    s_ff.nearer()
+    together((s_qkv, "one"), (s_qkv, "three"), (s_qkv, "block"), (s_in, "first"), (s_in, "third"), (s_ff, "block"))
     s_qkv.farther()
     s_in.nearer()
-    s_qkv.swap("one", "three")
-    together((s_qkv, "two"), (s_qkv, "other_three"), (s_qkv, "other_one"), (s_in, "block"), (s_ff, "block"))
+    s_qkv.swap("block", "one", "three")
+    together(
+        (s_qkv, "two"), (s_qkv, "other_block"), (s_qkv, "other_three"), (s_qkv, "other_one"),
+        (s_in, "block"), (s_ff, "block"),
+    )
     s_in.far_one()
     s_in.far_three()
     s_ff.far_one()
@@ -1113,10 +1111,11 @@
     together((v, "some"), (r_qkv, "one"), (r_qkv, "two"))
     r_qkv.far()
     v.hidden = hidden_back(v.some, w_qkv, rows_qkv)
-    together((v, "hidden"), (r_ff, "one"), (r_ff, "two"), (r_ff, "three"))
-    g_ff = r_ff.result().reshape(-1, rows_ff, width).transpose(1, 0, 2).reshape(rows_ff, -1)[:, :units]
-    v.g_ff = drop_units(g_ff, n, padded, w_in_rows)
-    together((v, "g_ff"), (v, "hidden"), (r_qkv, "one"), (r_qkv, "two"), (r_in, "one"), (r_in, "two"))
+    together(
+        (v, "hidden"), (r_qkv, "one"), (r_qkv, "two"), (r_in, "one"), (r_in, "two"),
+        (r_ff, "one"), (r_ff, "two"), (r_ff, "three"),
+    )
+    v.g_ff = drop_units(r_ff.result(), n, padded, w_in_rows)
     r_qkv.repack()
     together((v, "hidden"), (r_qkv, "three"))
     r_qkv.farther()

time: 433 us -> 427 us (0.986)
  transfers between devices with their start and end apart: 53 -> 53, of which waited for: 14 -> 15; matrix products, arithmetic and copies ran while one was open for 4% -> 5% of each run, Pallas kernels for 45% -> 45%
where the time goes in v1:
time: 427 us; the launch traced here: 420 us
  Pallas kernels  278 us (65%)
  starting transfers between devices  56.3 us (13%)
  waiting for transfers between devices  51.3 us (12%)
  other arithmetic  20.5 us (5%)
  local copies, waits for them, and re-layouts  12.6 us (3%)
    pallas_call x4, Pallas kernels, fetching_call(): return lambda *args: made(*[order for order, _ in weights], *pieces, *args)  123 us
    pallas_call x5, Pallas kernels, attend_back(): call(kernel, name='attend_back', grid=(number,), in_specs=[tall(0), tall(...  61.9 us
    ppermute x36, starting transfers between devices, hop(): return lax.ppermute(array, axis, pairs)  49.6 us
    ppermute x36, waiting for transfers between devices, hop(): return lax.ppermute(array, axis, pairs)  46.9 us
    pallas_call x9, Pallas kernels, collect_call(): pl.pallas_call(kernel, name=name, grid_spec=pltpu.PrefetchScalarGridSpec(...  39.1 us
    pallas_call x2, Pallas kernels, attend(): call(kernel, name='attend', grid=(number,), in_specs=[tall(0), tall(pairs...  32.6 us
    pallas_call x1, Pallas kernels, project_grad_halves(): pl.pallas_call(functools.partial(project_grad_halves_kernel, rows), name=...  13.6 us
  transfers between devices with their start and end apart: 53, of which 15 were waited for; matrix products, arithmetic and copies ran while one was open for 5% of the time, Pallas kernels for 45%

profile of v1, /device:TPU:0, one launch (start us, length us, event | category | flops | bytes accessed | tf_op | source)
XLA Modules:
  0.0 420.2 jit_solution(2140328557297074209)
XLA Ops:
  18.0 5.9 %collective-permute-done.1 = bf16[104,1024]{1,0:T(8,128)(2,1)S(1)} collective-permute-done((bf16[104,1024]{1,0:T(8,128)(2,1)S(1)}, bf16[104,1024]{1,0:T(8,128)(2,1)S(1)}, u32[]{:S(2)}, u32[]{:S(2)}) %collective-permute-start.1) | collective-permute-done | bytes 213024 | tf_op jit(solution)/shard_map/ppermute | solution.py:690
  28.4 3.8 collective-permute-start.8
  32.6 14.4 %collective-permute-done.9 = bf16[32,2816]{1,0:T(8,128)(2,1)S(1)} collective-permute-done((bf16[32,2816]{1,0:T(8,128)(2,1)S(1)}, bf16[32,2816]{1,0:T(8,128)(2,1)S(1)}, u32[]{:S(2)}, u32[]{:S(2)}) %collective-permute-start.9) | collective-permute-done | bytes 180256 | tf_op jit(solution)/shard_map/ppermute | solution.py:690
  50.1 14.0 %collective-permute-done.14 = bf16[208,1024]{1,0:T(8,128)(2,1)S(1)} collective-permute-done((bf16[208,1024]{1,0:T(8,128)(2,1)S(1)}, bf16[208,1024]{1,0:T(8,128)(2,1)S(1)}, u32[]{:S(2)}, u32[]{:S(2)}) %collective-permute-start.14) | collective-permute-done | bytes 426016 | tf_op jit(solution)/shard_map/ppermute | solution.py:690
  68.2 17.3 %norm_project.1 = (bf16[1024,3072]{1,0:T(8,128)(2,1)}, bf16[1024,1024]{1,0:T(8,128)(2,1)}, f32[2,1024]{1,0:T(2,128)}) custom-call(s32[32]{0:T(128)} %pad_add_fusion.3.refs_0_, bf16[4,104,1024]{2,1,0:T(8,128)(2,1)} %pad_maximum_fusion.1.refs_1_, bf16[4,104,1024]{2,1,0:T(8,128)(2,1)} %collective-permute-done.5.refs_2_, ...), custom_call_target="tpu_custom_call" | custom-call | flops 6442450944 | bytes 16777216 | tf_op jit(solution)/shard_map/norm_project/pallas_call | solution.py:144
  89.2 16.3 %attend.2 = (bf16[1024,1024]{1,0:T(8,128)(2,1)}, f32[8,2,1024]{2,1,0:T(2,128)}) custom-call(bf16[1024,3072]{1,0:T(8,128)(2,1)} %get-tuple-element.177.refs_0_.refs_1_.refs_2_, bf16[1024,3072]{1,0:T(8,128)(2,1)} %get-tuple-element.177.refs_0_.refs_1_.refs_2_, bf16[1024,3072]{1,0:T(8,128)(2,1)} %get-tuple-element.177.refs_0_.refs_1_.refs_2_, ...), custom_call_target="tpu_custom_call" | custom-call | flops 8589934592 | bytes 4194304 | tf_op jit(solution)/shard_map/attend/pallas_call | solution.py:258
  108.0 16.3 %attend.3 = (bf16[1024,1024]{1,0:T(8,128)(2,1)}, f32[8,2,1024]{2,1,0:T(2,128)}) custom-call(bf16[1024,3072]{1,0:T(8,128)(2,1)} %get-tuple-element.177.refs_0_.refs_1_.refs_2_, bf16[1024,3072]{1,0:T(8,128)(2,1)} %get-tuple-element.177.refs_0_.refs_1_.refs_2_, ...), custom_call_target="tpu_custom_call", output_to_operand_aliasing={{0}: (5, {}), {1}: (6, {})} | custom-call | flops 8589934592 | bytes 4194304 | tf_op jit(solution)/shard_map/attend/pallas_call | solution.py:258
  124.3 4.1 collective-permute-done.24.refs_12_.refs_3_
  135.6 78.2 %ffn_forward_backward.1 = (f32[1024,1024]{1,0:T(8,128)}, bf16[1024,2816]{1,0:T(8,128)(2,1)}, f32[1024,1024]{1,0:T(8,128)}, bf16[1024,1024]{1,0:T(8,128)(2,1)}, b...) custom-call(s32[32]{0:T(128)} %pad_add_fusion.3.refs_0_, ...), custom_call_target="tpu_custom_call" | custom-call | flops 47244640256 | bytes 55574528 | tf_op jit(solution)/shard_map/ffn_forward_backward/pallas_call | solution.py:144
  214.2 8.6 %attend_back.5.refs_10_ = bf16[3,1024,1024]{2,1,0:T(8,128)(2,1)} custom-call(bf16[1024,3072]{1,0:T(8,128)(2,1)} %get-tuple-element.177.refs_0_.refs_1_.refs_2_, bf16[1024,3072]{1,0:T(8,128)(2,1)} %get-tuple-element.177.refs_0_.refs_1_.refs_2_, bf16[1024,3072]{1,0:T(8,128)(2,1)} %get-tuple-element.177.refs_0_.refs_1_.refs_2_, ...), custom_call_target="tpu_custom_call" | custom-call | flops 5368709120 | bytes 2097152 | tf_op jit(solution)/shard_map/attend_back/pallas_call | solution.py:329
  226.5 3.9 collect_grads.6
  230.4 3.7 collective-permute-start.33
  234.1 14.7 %attend_back.6.refs_10_ = bf16[3,1024,1024]{2,1,0:T(8,128)(2,1)} custom-call(bf16[1024,3072]{1,0:T(8,128)(2,1)} %get-tuple-element.177.refs_0_.refs_1_.refs_2_, bf16[1024,3072]{1,0:T(8,128)(2,1)} %get-tuple-element.177.refs_0_.refs_1_.refs_2_, bf16[1024,3072]{1,0:T(8,128)(2,1)} %get-tuple-element.177.refs_0_.refs_1_.refs_2_, ...), custom_call_target="tpu_custom_call", output_to_operand_aliasing={{}: (10, {})} | custom-call | flops 10737418240 | bytes 4194304 | tf_op jit(solution)/shard_map/attend_back/pallas_call | solution.py:329
  248.9 5.9 %collect_grads.7 = (bf16[4,208,1024]{2,1,0:T(8,128)(2,1)}, bf16[4,208,1024]{2,1,0:T(8,128)(2,1)}) custom-call(s32[5,4]{1,0:T(8,128)} %concatenate.152.chosen_ref, bf16[32,176,1024]{2,1,0:T(8,128)(2,1)} %bitcast.134, bf16[32,176,1024]{2,1,0:T(8,128)(2,1)} %bitcast.135, bf16[32,176,1024]{2,1,0:T(8,128)(2,1)} %bitcast.136, bf16[32,176,1024]{2,1,0:T(8,128)(2,1)} %bitcast.137, ...), custom_call_target="tpu_custom_call" | custom-call | flops 10223616 | bytes 10223616 | tf_op jit(solution)/shard_map/collect_grads/pallas_call | solution.py:779
  256.9 14.9 %attend_back.7.refs_10_ = bf16[3,1024,1024]{2,1,0:T(8,128)(2,1)} custom-call(bf16[1024,3072]{1,0:T(8,128)(2,1)} %get-tuple-element.177.refs_0_.refs_1_.refs_2_, bf16[1024,3072]{1,0:T(8,128)(2,1)} %get-tuple-element.177.refs_0_.refs_1_.refs_2_, bf16[1024,3072]{1,0:T(8,128)(2,1)} %get-tuple-element.177.refs_0_.refs_1_.refs_2_, ...), custom_call_target="tpu_custom_call", output_to_operand_aliasing={{}: (10, {})} | custom-call | flops 10737418240 | bytes 4194304 | tf_op jit(solution)/shard_map/attend_back/pallas_call | solution.py:329
  271.8 3.5 collect_grads.8
  275.3 3.8 collective-permute-start.37
  279.1 15.0 %attend_back.8.refs_10_ = bf16[3,1024,1024]{2,1,0:T(8,128)(2,1)} custom-call(bf16[1024,3072]{1,0:T(8,128)(2,1)} %get-tuple-element.177.refs_0_.refs_1_.refs_2_, bf16[1024,3072]{1,0:T(8,128)(2,1)} %get-tuple-element.177.refs_0_.refs_1_.refs_2_, bf16[1024,3072]{1,0:T(8,128)(2,1)} %get-tuple-element.177.refs_0_.refs_1_.refs_2_, ...), custom_call_target="tpu_custom_call", output_to_operand_aliasing={{}: (10, {})} | custom-call | flops 10737418240 | bytes 4194304 | tf_op jit(solution)/shard_map/attend_back/pallas_call | solution.py:329
  295.2 5.0 %collect_grads.9 = bf16[4,208,1024]{2,1,0:T(8,128)(2,1)} custom-call(s32[5,4]{1,0:T(8,128)} %concatenate.152.chosen_ref, bf16[32,176,1024]{2,1,0:T(8,128)(2,1)} %bitcast.138, bf16[32,176,1024]{2,1,0:T(8,128)(2,1)} %bitcast.139, bf16[32,176,1024]{2,1,0:T(8,128)(2,1)} %bitcast.140, bf16[32,176,1024]{2,1,0:T(8,128)(2,1)} %bitcast.141, ...), custom_call_target="tpu_custom_call" | custom-call | flops 6815744 | bytes 6815744 | tf_op jit(solution)/shard_map/collect_grads/pallas_call | solution.py:779
  300.9 8.7 %attend_back.9.gp_ref.refs_9_ = bf16[3,1024,1024]{2,1,0:T(8,128)(2,1)} custom-call(bf16[1024,3072]{1,0:T(8,128)(2,1)} %get-tuple-element.177.refs_0_.refs_1_.refs_2_, bf16[1024,3072]{1,0:T(8,128)(2,1)} %get-tuple-element.177.refs_0_.refs_1_.refs_2_, bf16[1024,3072]{1,0:T(8,128)(2,1)} %get-tuple-element.177.refs_0_.refs_1_.refs_2_, ...), custom_call_target="tpu_custom_call", output_to_operand_aliasing={{}: (10, {})} | custom-call | flops 5368709120 | bytes 2097152 | tf_op jit(solution)/shard_map/attend_back/pallas_call | solution.py:329
  309.6 3.7 collect_last_grads.3
  316.8 13.6 %grad_qkv.1 = (bf16[1536,1024]{1,0:T(8,128)(2,1)}, bf16[1536,1024]{1,0:T(8,128)(2,1)}) custom-call(s32[1]{0:T(128)} %bitcast.120.core_ref, bf16[3,1024,1024]{2,1,0:T(8,128)(2,1)} %attend_back.9.gp_ref.refs_9_, bf16[1024,1024]{1,0:T(8,128)(2,1)} %get-tuple-element.241.hid_ref), custom_call_target="tpu_custom_call" | custom-call | flops 6442450944 | bytes 14680064 | tf_op jit(solution)/shard_map/grad_qkv/pallas_call | solution.py:567
  331.1 5.5 %collect_last_grads.4 = (bf16[208,1024]{1,0:T(8,128)(2,1)}, bf16[208,1024]{1,0:T(8,128)(2,1)}, f32[208,1024]{1,0:T(8,128)}, f32[208,1024]{1,0:T(8,128)}) custom-call(s32[5,4]{1,0:T(8,128)} %concatenate.152.chosen_ref, bf16[32,176,1024]{2,1,0:T(8,128)(2,1)} %bitcast.142, bf16[32,176,1024]{2,1,0:T(8,128)(2,1)} %bitcast.143, bf16[32,176,1024]{2,1,0:T(8,128)(2,1)} %bitcast.144, ...), custom_call_target="tpu_custom_call" | custom-call | flops 10223616 | bytes 10223616 | tf_op jit(solution)/shard_map/collect_last_grads/pallas_call | solution.py:779
  336.7 4.1 collect_grads.10
  344.0 3.8 collective-permute-start.45
  347.9 15.2 %grad_hidden_one.1.grad_ref = f32[1024,1024]{1,0:T(8,128)} custom-call(s32[32]{0:T(128)} %pad_add_fusion.3.refs_0_, bf16[4,104,1024]{2,1,0:T(8,128)(2,1)} %pad_maximum_fusion.1.refs_1_, bf16[4,104,1024]{2,1,0:T(8,128)(2,1)} %collective-permute-done.5.refs_2_, bf16[4,104,1024]{2,1,0:T(8,128)(2,1)} %collective-permute-done.10.refs_3_, ...), custom_call_target="tpu_custom_call" | custom-call | flops 6442450944 | bytes 16777216 | tf_op jit(solution)/shard_map/grad_hidden_one/pallas_call | solution.py:144
  363.0 4.1 collective-permute-done.46
  368.0 3.6 collect_grads.11
  379.7 7.6 %grad_tokens.1 = (f32[1024,1024]{1,0:T(8,128)}, f32[1,1024]{1,0:T(1,128)}) custom-call(f32[1024,1024]{1,0:T(8,128)} %grad_hidden_one.1.grad_ref, bf16[1024,1024]{1,0:T(8,128)(2,1)} %tok_ref.1, f32[1024,1024]{1,0:T(8,128)} %get-tuple-element.271.mid_ref, f32[2,1024]{1,0:T(2,128)} %get-tuple-element.201.refs_21_.gain_ref), custom_call_target="tpu_custom_call" | custom-call | flops 20971520 | bytes 14680064 | tf_op jit(solution)/shard_map/grad_tokens/pallas_call | solution.py:645
  389.4 3.5 all-to-all-start
  392.8 3.8 collect_last_grads.5
  403.1 12.6 %ffn_output.1 = bf16[1024,1024]{1,0:T(8,128)(2,1)} custom-call(s32[32]{0:T(128)} %pad_add_fusion.2.refs_1_.refs_0_, bf16[4,32,2816]{2,1,0:T(8,128)(2,1)} %pad_maximum_fusion.2.refs_10_.refs_1_, bf16[4,32,2816]{2,1,0:T(8,128)(2,1)} %collective-permute-done.16.refs_11_.refs_2_, bf16[4,32,2816]{2,1,0:T(8,128)(2,1)} %collective-permute-done.24.refs_12_.refs_3_, ...), custom_call_target="tpu_custom_call" | custom-call | flops 5905580032 | bytes 17825792 | tf_op jit(solution)/shard_map/ffn_output/pallas_call | solution.py:144
  (202 shorter events, 79.5 us)
Async XLA Ops:
  25.9 22.1 %collective-permute-start.5 = (bf16[4,104,1024]{2,1,0:T(8,128)(2,1)}, bf16[4,104,1024]{2,1,0:T(8,128)(2,1)}, u32[]{:S(2)}, u32[]{:S(2)}) collective-permute-start(bf16[4,104,1024]{2,1,0:T(8,128)(2,1)} %pad_maximum_fusion.1.refs_1_), channel_id=1, source_target_pairs={{0,4},{1,3},{2,6},{3,1},{4,0},{5,7},{6,2},{7,5},{8,12},{9,11},{10,... | collective-permute-start | bytes 2555912 | tf_op jit(solution)/shard_map/ppermute | solution.py:690
  26.4 21.6 %collective-permute-start.6 = (bf16[4,104,1024]{2,1,0:T(8,128)(2,1)}, bf16[4,104,1024]{2,1,0:T(8,128)(2,1)}, u32[]{:S(2)}, u32[]{:S(2)}) collective-permute-start(bf16[4,104,1024]{2,1,0:T(8,128)(2,1)} %pad_maximum_fusion.1.refs_1_), channel_id=1, source_target_pairs={{0,2},{1,5},{2,0},{3,7},{4,6},{5,1},{6,4},{7,3},{8,10},{9,13},{10,... | collective-permute-start | bytes 2555912 | tf_op jit(solution)/shard_map/ppermute | solution.py:690
  26.9 20.0 %collective-permute-start.9 = (bf16[32,2816]{1,0:T(8,128)(2,1)S(1)}, bf16[32,2816]{1,0:T(8,128)(2,1)S(1)}, u32[]{:S(2)}, u32[]{:S(2)}) collective-permute-start(bf16[32,2816]{1,0:T(8,128)(2,1)S(1)} %collective-permute-done.3), channel_id=1, source_target_pairs={{0,4},{1,3},{2,6},{3,1},{4,0},{5,7},{6,2},{7,5},{8,12},{9,11},{10,... | collective-permute-start | bytes 540680 | tf_op jit(solution)/shard_map/ppermute | solution.py:690
  28.4 19.5 %collective-permute-start.7 = (bf16[208,1024]{1,0:T(8,128)(2,1)S(1)}, bf16[208,1024]{1,0:T(8,128)(2,1)S(1)}, u32[]{:S(2)}, u32[]{:S(2)}) collective-permute-start(bf16[208,1024]{1,0:T(8,128)(2,1)S(1)} %fusion.1), channel_id=1, source_target_pairs={{0,8},{1,9},{2,10},{3,11},{4,12},{5,13},{6,14},{7,15},{8,16},{9,17... | collective-permute-start | bytes 1277960 | tf_op jit(solution)/shard_map/ppermute | solution.py:690
  28.4 19.5 %collective-permute-start.8 = (bf16[208,1024]{1,0:T(8,128)(2,1)S(1)}, bf16[208,1024]{1,0:T(8,128)(2,1)S(1)}, u32[]{:S(2)}, u32[]{:S(2)}) collective-permute-start(bf16[208,1024]{1,0:T(8,128)(2,1)S(1)} %fusion.1), channel_id=1, source_target_pairs={{0,24},{1,25},{2,26},{3,27},{4,28},{5,29},{6,30},{7,31},{8,0},{9,1... | collective-permute-start | bytes 1277960 | tf_op jit(solution)/shard_map/ppermute | solution.py:690
  47.9 17.4 %collective-permute-start.10 = (bf16[4,104,1024]{2,1,0:T(8,128)(2,1)}, bf16[4,104,1024]{2,1,0:T(8,128)(2,1)}, u32[]{:S(2)}, u32[]{:S(2)}) collective-permute-start(bf16[4,104,1024]{2,1,0:T(8,128)(2,1)} %collective-permute-done.5.refs_2_), channel_id=1, source_target_pairs={{0,2},{1,5},{2,0},{3,7},{4,6},{5,1},{6,4},{7,3},{8,10},{9,13},{10,... | collective-permute-start | bytes 2555912 | tf_op jit(solution)/shard_map/ppermute | solution.py:690
  66.1 20.6 %collective-permute-start.16 = (bf16[4,32,2816]{2,1,0:T(8,128)(2,1)}, bf16[4,32,2816]{2,1,0:T(8,128)(2,1)}, u32[]{:S(2)}, u32[]{:S(2)}) collective-permute-start(bf16[4,32,2816]{2,1,0:T(8,128)(2,1)} %pad_maximum_fusion.2.refs_10_.refs_1_), channel_id=1, source_target_pairs={{0,8},{1,9},{2,10},{3,11},{4,12},{5,13},{6,14},{7,15},{8,16},{9,17... | collective-permute-start | bytes 2162696 | tf_op jit(solution)/shard_map/ppermute | solution.py:690
  66.4 20.4 %collective-permute-start.17 = (bf16[4,32,2816]{2,1,0:T(8,128)(2,1)}, bf16[4,32,2816]{2,1,0:T(8,128)(2,1)}, u32[]{:S(2)}, u32[]{:S(2)}) collective-permute-start(bf16[4,32,2816]{2,1,0:T(8,128)(2,1)} %pad_maximum_fusion.2.refs_10_.refs_1_), channel_id=1, source_target_pairs={{0,1},{1,0},{2,3},{3,2},{4,5},{5,4},{6,7},{7,6},{8,9},{9,8},{10,11... | collective-permute-start | bytes 2162696 | tf_op jit(solution)/shard_map/ppermute | solution.py:694
  67.4 39.7 %collective-permute-start.18 = (bf16[4,208,1024]{2,1,0:T(8,128)(2,1)S(1)}, bf16[4,208,1024]{2,1,0:T(8,128)(2,1)}, u32[]{:S(2)}, u32[]{:S(2)}) collective-permute-start(bf16[4,208,1024]{2,1,0:T(8,128)(2,1)S(1)} %pad_maximum_fusion.refs_2_), channel_id=1, source_target_pairs={{0,4},{1,3},{2,6},{3,1},{4,0},{5,7},{6,2},{7,5},{8,12},{9,11},{10,... | collective-permute-start | bytes 5111816 | tf_op jit(solution)/shard_map/ppermute | solution.py:690
  67.7 39.3 %collective-permute-start.19 = (bf16[4,208,1024]{2,1,0:T(8,128)(2,1)S(1)}, bf16[4,208,1024]{2,1,0:T(8,128)(2,1)}, u32[]{:S(2)}, u32[]{:S(2)}) collective-permute-start(bf16[4,208,1024]{2,1,0:T(8,128)(2,1)S(1)} %pad_maximum_fusion.refs_2_), channel_id=1, source_target_pairs={{0,2},{1,5},{2,0},{3,7},{4,6},{5,1},{6,4},{7,3},{8,10},{9,13},{10,... | collective-permute-start | bytes 5111816 | tf_op jit(solution)/shard_map/ppermute | solution.py:690
  86.8 20.2 %collective-permute-start.21 = (bf16[4,208,1024]{2,1,0:T(8,128)(2,1)S(1)}, bf16[4,208,1024]{2,1,0:T(8,128)(2,1)}, u32[]{:S(2)}, u32[]{:S(2)}) collective-permute-start(bf16[4,208,1024]{2,1,0:T(8,128)(2,1)S(1)} %pad_maximum_fusion.refs_2_), channel_id=1, source_target_pairs={{0,1},{1,0},{2,3},{3,2},{4,5},{5,4},{6,7},{7,6},{8,9},{9,8},{10,11... | collective-permute-start | bytes 5111816 | tf_op jit(solution)/shard_map/ppermute | solution.py:694
  86.8 18.9 %collective-permute-start.20 = (bf16[4,32,2816]{2,1,0:T(8,128)(2,1)}, bf16[4,32,2816]{2,1,0:T(8,128)(2,1)}, u32[]{:S(2)}, u32[]{:S(2)}) collective-permute-start(bf16[4,32,2816]{2,1,0:T(8,128)(2,1)} %pad_maximum_fusion.2.refs_10_.refs_1_), channel_id=1, source_target_pairs={{0,24},{1,25},{2,26},{3,27},{4,28},{5,29},{6,30},{7,31},{8,0},{9,1... | collective-permute-start | bytes 2162696 | tf_op jit(solution)/shard_map/ppermute | solution.py:690
  107.0 22.0 %collective-permute-start.23 = (bf16[4,208,1024]{2,1,0:T(8,128)(2,1)}, bf16[4,208,1024]{2,1,0:T(8,128)(2,1)S(1)}, u32[]{:S(2)}, u32[]{:S(2)}) collective-permute-start(bf16[4,208,1024]{2,1,0:T(8,128)(2,1)} %collective-permute-done.18.refs_3_), channel_id=1, source_target_pairs={{0,2},{1,5},{2,0},{3,7},{4,6},{5,1},{6,4},{7,3},{8,10},{9,13},{10,... | collective-permute-start | bytes 5111816 | tf_op jit(solution)/shard_map/ppermute | solution.py:690
  107.5 21.6 %collective-permute-start.25 = (bf16[4,208,1024]{2,1,0:T(8,128)(2,1)}, bf16[4,208,1024]{2,1,0:T(8,128)(2,1)}, u32[]{:S(2)}, u32[]{:S(2)}) collective-permute-start(bf16[4,208,1024]{2,1,0:T(8,128)(2,1)} %collective-permute-done.18.refs_3_), channel_id=1, source_target_pairs={{0,1},{1,0},{2,3},{3,2},{4,5},{5,4},{6,7},{7,6},{8,9},{9,8},{10,11... | collective-permute-start | bytes 5111816 | tf_op jit(solution)/shard_map/ppermute | solution.py:694
  107.5 21.6 %collective-permute-start.26 = (bf16[4,208,1024]{2,1,0:T(8,128)(2,1)}, bf16[4,208,1024]{2,1,0:T(8,128)(2,1)}, u32[]{:S(2)}, u32[]{:S(2)}) collective-permute-start(bf16[4,208,1024]{2,1,0:T(8,128)(2,1)} %collective-permute-done.19.refs_5_), channel_id=1, source_target_pairs={{0,1},{1,0},{2,3},{3,2},{4,5},{5,4},{6,7},{7,6},{8,9},{9,8},{10,11... | collective-permute-start | bytes 5111816 | tf_op jit(solution)/shard_map/ppermute | solution.py:694
  108.0 20.4 %collective-permute-start.24 = (bf16[4,32,2816]{2,1,0:T(8,128)(2,1)}, bf16[4,32,2816]{2,1,0:T(8,128)(2,1)}, u32[]{:S(2)}, u32[]{:S(2)}) collective-permute-start(bf16[4,32,2816]{2,1,0:T(8,128)(2,1)} %collective-permute-done.16.refs_11_.refs_2_), channel_id=1, source_target_pairs={{0,8},{1,9},{2,10},{3,11},{4,12},{5,13},{6,14},{7,15},{8,16},{9,17... | collective-permute-start | bytes 2162696 | tf_op jit(solution)/shard_map/ppermute | solution.py:690
  108.0 20.4 %collective-permute-start.27 = (bf16[4,32,2816]{2,1,0:T(8,128)(2,1)}, bf16[4,32,2816]{2,1,0:T(8,128)(2,1)}, u32[]{:S(2)}, u32[]{:S(2)}) collective-permute-start(bf16[4,32,2816]{2,1,0:T(8,128)(2,1)} %collective-permute-done.20.refs_13_.refs_4_), channel_id=1, source_target_pairs={{0,1},{1,0},{2,3},{3,2},{4,5},{5,4},{6,7},{7,6},{8,9},{9,8},{10,11... | collective-permute-start | bytes 2162696 | tf_op jit(solution)/shard_map/ppermute | solution.py:694
  223.6 25.2 %collective-permute-start.31 = (bf16[32,176,1024]{2,1,0:T(8,128)(2,1)}, bf16[32,176,1024]{2,1,0:T(8,128)(2,1)}, u32[]{:S(2)}, u32[]{:S(2)}) collective-permute-start(bf16[32,176,1024]{2,1,0:T(8,128)(2,1)} %bitcast.133), channel_id=1, source_target_pairs={{0,1},{1,0},{2,3},{3,2},{4,5},{5,4},{6,7},{7,6},{8,9},{9,8},{10,11... | collective-permute-start | bytes 34603016 | tf_op jit(solution)/shard_map/ppermute | solution.py:694
  224.0 24.9 %collective-permute-start.32 = (bf16[32,32,1024]{2,1,0:T(8,128)(2,1)}, bf16[32,32,1024]{2,1,0:T(8,128)(2,1)}, u32[]{:S(2)}, u32[]{:S(2)}) collective-permute-start(bf16[32,32,1024]{2,1,0:T(8,128)(2,1)} %bitcast.171), channel_id=1, source_target_pairs={{0,1},{1,0},{2,3},{3,2},{4,5},{5,4},{6,7},{7,6},{8,9},{9,8},{10,11... | collective-permute-start | bytes 6291464 | tf_op jit(solution)/shard_map/ppermute | solution.py:694
  230.4 41.4 %collective-permute-start.33 = (bf16[4,32,2816]{2,1,0:T(8,128)(2,1)}, bf16[4,32,2816]{2,1,0:T(8,128)(2,1)}, u32[]{:S(2)}, u32[]{:S(2)}) collective-permute-start(bf16[4,32,2816]{2,1,0:T(8,128)(2,1)} %get-tuple-element.222), channel_id=1, source_target_pairs={{0,24},{1,25},{2,26},{3,27},{4,28},{5,29},{6,30},{7,31},{8,0},{9,1... | collective-permute-start | bytes 2162696 | tf_op jit(solution)/shard_map/ppermute | solution.py:690
  234.1 37.7 %collective-permute-start.34 = (bf16[4,32,2816]{2,1,0:T(8,128)(2,1)}, bf16[4,32,2816]{2,1,0:T(8,128)(2,1)}, u32[]{:S(2)}, u32[]{:S(2)}) collective-permute-start(bf16[4,32,2816]{2,1,0:T(8,128)(2,1)} %get-tuple-element.223), channel_id=1, source_target_pairs={{0,8},{1,9},{2,10},{3,11},{4,12},{5,13},{6,14},{7,15},{8,16},{9,17... | collective-permute-start | bytes 2162696 | tf_op jit(solution)/shard_map/ppermute | solution.py:690
  254.8 39.5 %collective-permute-start.35 = (bf16[4,208,1024]{2,1,0:T(8,128)(2,1)}, bf16[4,208,1024]{2,1,0:T(8,128)(2,1)}, u32[]{:S(2)}, u32[]{:S(2)}) collective-permute-start(bf16[4,208,1024]{2,1,0:T(8,128)(2,1)} %get-tuple-element.227), channel_id=1, source_target_pairs={{0,2},{1,5},{2,0},{3,7},{4,6},{5,1},{6,4},{7,3},{8,10},{9,13},{10,... | collective-permute-start | bytes 5111816 | tf_op jit(solution)/shard_map/ppermute | solution.py:690
  255.5 39.7 %collective-permute-start.36 = (bf16[4,208,1024]{2,1,0:T(8,128)(2,1)}, bf16[4,208,1024]{2,1,0:T(8,128)(2,1)S(1)}, u32[]{:S(2)}, u32[]{:S(2)}) collective-permute-start(bf16[4,208,1024]{2,1,0:T(8,128)(2,1)} %get-tuple-element.228), channel_id=1, source_target_pairs={{0,2},{1,5},{2,0},{3,7},{4,6},{5,1},{6,4},{7,3},{8,10},{9,13},{10,... | collective-permute-start | bytes 5111816 | tf_op jit(solution)/shard_map/ppermute | solution.py:690
  275.3 19.0 %collective-permute-start.37 = (bf16[4,32,2816]{2,1,0:T(8,128)(2,1)}, bf16[4,32,2816]{2,1,0:T(8,128)(2,1)}, u32[]{:S(2)}, u32[]{:S(2)}) collective-permute-start(bf16[4,32,2816]{2,1,0:T(8,128)(2,1)} %collect_grads.8), channel_id=1, source_target_pairs={{0,24},{1,25},{2,26},{3,27},{4,28},{5,29},{6,30},{7,31},{8,0},{9,1... | collective-permute-start | bytes 2162696 | tf_op jit(solution)/shard_map/ppermute | solution.py:690
  300.2 30.2 %collective-permute-start.38 = (bf16[4,208,1024]{2,1,0:T(8,128)(2,1)}, bf16[4,208,1024]{2,1,0:T(8,128)(2,1)}, u32[]{:S(2)}, u32[]{:S(2)}) collective-permute-start(bf16[4,208,1024]{2,1,0:T(8,128)(2,1)} %collect_grads.9), channel_id=1, source_target_pairs={{0,4},{1,3},{2,6},{3,1},{4,0},{5,7},{6,2},{7,5},{8,12},{9,11},{10,... | collective-permute-start | bytes 5111816 | tf_op jit(solution)/shard_map/ppermute | solution.py:690
  313.2 17.1 %collective-permute-start.39 = (bf16[32,2816]{1,0:T(8,128)(2,1)}, bf16[32,2816]{1,0:T(8,128)(2,1)S(1)}, u32[]{:S(2)}, u32[]{:S(2)}) collective-permute-start(bf16[32,2816]{1,0:T(8,128)(2,1)} %get-tuple-element.245), channel_id=1, source_target_pairs={{0,6},{1,7},{2,4},{3,5},{4,2},{5,3},{6,0},{7,1},{8,14},{9,15},{10,... | collective-permute-start | bytes 540680 | tf_op jit(solution)/shard_map/ppermute | solution.py:690
  340.8 26.3 %collective-permute-start.43 = (bf16[4,96,1024]{2,1,0:T(8,128)(2,1)}, bf16[4,96,1024]{2,1,0:T(8,128)(2,1)S(1)}, u32[]{:S(2)}, u32[]{:S(2)}) collective-permute-start(bf16[4,96,1024]{2,1,0:T(8,128)(2,1)} %get-tuple-element.260), channel_id=1, source_target_pairs={{0,2},{1,5},{2,0},{3,7},{4,6},{5,1},{6,4},{7,3},{8,10},{9,13},{10,... | collective-permute-start | bytes 2359304 | tf_op jit(solution)/shard_map/ppermute | solution.py:690
  342.4 24.7 %collective-permute-start.44 = (bf16[4,96,1024]{2,1,0:T(8,128)(2,1)}, bf16[4,96,1024]{2,1,0:T(8,128)(2,1)S(1)}, u32[]{:S(2)}, u32[]{:S(2)}) collective-permute-start(bf16[4,96,1024]{2,1,0:T(8,128)(2,1)} %get-tuple-element.261), channel_id=1, source_target_pairs={{0,2},{1,5},{2,0},{3,7},{4,6},{5,1},{6,4},{7,3},{8,10},{9,13},{10,... | collective-permute-start | bytes 2359304 | tf_op jit(solution)/shard_map/ppermute | solution.py:690
  344.0 19.0 %collective-permute-start.45 = (bf16[208,1024]{1,0:T(8,128)(2,1)}, bf16[208,1024]{1,0:T(8,128)(2,1)}, u32[]{:S(2)}, u32[]{:S(2)}) collective-permute-start(bf16[208,1024]{1,0:T(8,128)(2,1)} %get-tuple-element.262), channel_id=1, source_target_pairs={{0,24},{1,25},{2,26},{3,27},{4,28},{5,29},{6,30},{7,31},{8,0},{9,1... | collective-permute-start | bytes 1277960 | tf_op jit(solution)/shard_map/ppermute | solution.py:690
  347.9 19.2 %collective-permute-start.46 = (bf16[208,1024]{1,0:T(8,128)(2,1)}, bf16[208,1024]{1,0:T(8,128)(2,1)S(1)}, u32[]{:S(2)}, u32[]{:S(2)}) collective-permute-start(bf16[208,1024]{1,0:T(8,128)(2,1)} %get-tuple-element.263), channel_id=1, source_target_pairs={{0,8},{1,9},{2,10},{3,11},{4,12},{5,13},{6,14},{7,15},{8,16},{9,17... | collective-permute-start | bytes 1277960 | tf_op jit(solution)/shard_map/ppermute | solution.py:690
  389.4 26.4 %all-to-all-start = ((f32[32,2,32]{2,1,0:T(2,128)}), f32[32,2,32]{2,1,0:T(2,128)S(1)}, u32[]{:S(2)}, u32[]{:S(2)}) async-start(f32[32,2,32]{2,1,0:T(2,128)} %pad_maximum_fusion.5), calls=%async_computation | async-start | bytes 65536 | tf_op jit(solution)/shard_map/all_to_all | solution.py:968
  396.6 19.7 %collective-permute-start.49 = (bf16[96,1024]{1,0:T(8,128)(2,1)}, bf16[96,1024]{1,0:T(8,128)(2,1)S(1)}, u32[]{:S(2)}, u32[]{:S(2)}) collective-permute-start(bf16[96,1024]{1,0:T(8,128)(2,1)} %get-tuple-element.283), channel_id=1, source_target_pairs={{0,16},{1,17},{2,18},{3,19},{4,20},{5,21},{6,22},{7,23},{8,24},{9,... | collective-permute-start | bytes 589832 | tf_op jit(solution)/shard_map/ppermute | solution.py:690
  (49 other events, 451.2 us)

commit v2 on v1

--- a/solution.py
+++ b/solution.py
@@ -641,11 +641,11 @@
 
 def norm_back(grad, tokens, mid, gain):
     count, width = tokens.shape
-    rows = pl.BlockSpec((256, width), lambda i: (i, 0))
+    rows = pl.BlockSpec((512, width), lambda i: (i, 0))
     return call(
         norm_back_kernel,
         name="grad_tokens",
-        grid=(count // 256,),
+        grid=(count // 512,),
         in_specs=[rows, rows, rows, whole((2, width))],
         out_specs=[rows, whole((1, width))],
         out_shape=[sds((count, width), F32), sds((1, width), F32)],
@@ -1111,15 +1111,13 @@
     together((v, "some"), (r_qkv, "one"), (r_qkv, "two"))
     r_qkv.far()
     v.hidden = hidden_back(v.some, w_qkv, rows_qkv)
-    together(
-        (v, "hidden"), (r_qkv, "one"), (r_qkv, "two"), (r_in, "one"), (r_in, "two"),
-        (r_ff, "one"), (r_ff, "two"), (r_ff, "three"),
-    )
+    together((v, "hidden"), (r_in, "one"), (r_in, "two"))
+    r_in.nearer()
+    together((v, "hidden"), (r_qkv, "one"), (r_qkv, "two"), (r_ff, "one"), (r_ff, "two"), (r_ff, "three"))
     v.g_ff = drop_units(r_ff.result(), n, padded, w_in_rows)
     r_qkv.repack()
     together((v, "hidden"), (r_qkv, "three"))
     r_qkv.farther()
-    r_in.nearer()
     v.grad_tokens, v.g_one = norm_back(v.hidden, tokens, mid, v.gains)
     together((v, "grad_tokens"), (v, "g_one"), (r_qkv, "three"), (r_in, "three"))
     r_qkv.gather()

time: 427 us -> 427 us (level)
  transfers between devices with their start and end apart: 53 -> 53, of which waited for: 15 -> 15; matrix products, arithmetic and copies ran while one was open for 5% -> 5% of each run, Pallas kernels for 45% -> 44%
where the time goes in v2:
time: 427 us; the launch traced here: 420 us
  Pallas kernels  278 us (65%)
  starting transfers between devices  56.5 us (13%)
  waiting for transfers between devices  51.3 us (12%)
  other arithmetic  20.5 us (5%)
  local copies, waits for them, and re-layouts  12.6 us (3%)
    pallas_call x4, Pallas kernels, fetching_call(): return lambda *args: made(*[order for order, _ in weights], *pieces, *args)  123 us
    pallas_call x5, Pallas kernels, attend_back(): call(kernel, name='attend_back', grid=(number,), in_specs=[tall(0), tall(...  61.9 us
    ppermute x36, starting transfers between devices, hop(): return lax.ppermute(array, axis, pairs)  49.6 us
    ppermute x36, waiting for transfers between devices, hop(): return lax.ppermute(array, axis, pairs)  46.9 us
    pallas_call x9, Pallas kernels, collect_call(): pl.pallas_call(kernel, name=name, grid_spec=pltpu.PrefetchScalarGridSpec(...  39.1 us
    pallas_call x2, Pallas kernels, attend(): call(kernel, name='attend', grid=(number,), in_specs=[tall(0), tall(pairs...  32.6 us
    pallas_call x1, Pallas kernels, project_grad_halves(): pl.pallas_call(functools.partial(project_grad_halves_kernel, rows), name=...  13.6 us
  transfers between devices with their start and end apart: 53, of which 15 were waited for; matrix products, arithmetic and copies ran while one was open for 5% of the time, Pallas kernels for 44%

profile of v2, /device:TPU:0, one launch (start us, length us, event | category | flops | bytes accessed | tf_op | source)
XLA Modules:
  0.0 420.2 jit_solution(5479016733070231684)
XLA Ops:
  18.0 5.9 %collective-permute-done.1 = bf16[104,1024]{1,0:T(8,128)(2,1)S(1)} collective-permute-done((bf16[104,1024]{1,0:T(8,128)(2,1)S(1)}, bf16[104,1024]{1,0:T(8,128)(2,1)S(1)}, u32[]{:S(2)}, u32[]{:S(2)}) %collective-permute-start.1) | collective-permute-done | bytes 213024 | tf_op jit(solution)/shard_map/ppermute | solution.py:690
  28.4 3.8 collective-permute-start.8
  32.6 14.4 %collective-permute-done.9 = bf16[32,2816]{1,0:T(8,128)(2,1)S(1)} collective-permute-done((bf16[32,2816]{1,0:T(8,128)(2,1)S(1)}, bf16[32,2816]{1,0:T(8,128)(2,1)S(1)}, u32[]{:S(2)}, u32[]{:S(2)}) %collective-permute-start.9) | collective-permute-done | bytes 180256 | tf_op jit(solution)/shard_map/ppermute | solution.py:690
  50.1 14.0 %collective-permute-done.14 = bf16[208,1024]{1,0:T(8,128)(2,1)S(1)} collective-permute-done((bf16[208,1024]{1,0:T(8,128)(2,1)S(1)}, bf16[208,1024]{1,0:T(8,128)(2,1)S(1)}, u32[]{:S(2)}, u32[]{:S(2)}) %collective-permute-start.14) | collective-permute-done | bytes 426016 | tf_op jit(solution)/shard_map/ppermute | solution.py:690
  68.2 17.3 %norm_project.1 = (bf16[1024,3072]{1,0:T(8,128)(2,1)}, bf16[1024,1024]{1,0:T(8,128)(2,1)}, f32[2,1024]{1,0:T(2,128)}) custom-call(s32[32]{0:T(128)} %pad_add_fusion.3.refs_0_, bf16[4,104,1024]{2,1,0:T(8,128)(2,1)} %pad_maximum_fusion.1.refs_1_, bf16[4,104,1024]{2,1,0:T(8,128)(2,1)} %collective-permute-done.5.refs_2_, ...), custom_call_target="tpu_custom_call" | custom-call | flops 6442450944 | bytes 16777216 | tf_op jit(solution)/shard_map/norm_project/pallas_call | solution.py:144
  89.2 16.3 %attend.2 = (bf16[1024,1024]{1,0:T(8,128)(2,1)}, f32[8,2,1024]{2,1,0:T(2,128)}) custom-call(bf16[1024,3072]{1,0:T(8,128)(2,1)} %get-tuple-element.178.refs_0_.refs_1_.refs_2_, bf16[1024,3072]{1,0:T(8,128)(2,1)} %get-tuple-element.178.refs_0_.refs_1_.refs_2_, bf16[1024,3072]{1,0:T(8,128)(2,1)} %get-tuple-element.178.refs_0_.refs_1_.refs_2_, ...), custom_call_target="tpu_custom_call" | custom-call | flops 8589934592 | bytes 4194304 | tf_op jit(solution)/shard_map/attend/pallas_call | solution.py:258
  108.0 16.3 %attend.3 = (bf16[1024,1024]{1,0:T(8,128)(2,1)}, f32[8,2,1024]{2,1,0:T(2,128)}) custom-call(bf16[1024,3072]{1,0:T(8,128)(2,1)} %get-tuple-element.178.refs_0_.refs_1_.refs_2_, bf16[1024,3072]{1,0:T(8,128)(2,1)} %get-tuple-element.178.refs_0_.refs_1_.refs_2_, ...), custom_call_target="tpu_custom_call", output_to_operand_aliasing={{0}: (5, {}), {1}: (6, {})} | custom-call | flops 8589934592 | bytes 4194304 | tf_op jit(solution)/shard_map/attend/pallas_call | solution.py:258
  124.3 4.1 collective-permute-done.24.refs_12_.refs_3_
  135.6 78.2 %ffn_forward_backward.1 = (f32[1024,1024]{1,0:T(8,128)}, bf16[1024,2816]{1,0:T(8,128)(2,1)}, f32[1024,1024]{1,0:T(8,128)}, bf16[1024,1024]{1,0:T(8,128)(2,1)}, b...) custom-call(s32[32]{0:T(128)} %pad_add_fusion.3.refs_0_, ...), custom_call_target="tpu_custom_call" | custom-call | flops 47244640256 | bytes 55574528 | tf_op jit(solution)/shard_map/ffn_forward_backward/pallas_call | solution.py:144
  214.2 8.6 %attend_back.5.refs_10_ = bf16[3,1024,1024]{2,1,0:T(8,128)(2,1)} custom-call(bf16[1024,3072]{1,0:T(8,128)(2,1)} %get-tuple-element.178.refs_0_.refs_1_.refs_2_, bf16[1024,3072]{1,0:T(8,128)(2,1)} %get-tuple-element.178.refs_0_.refs_1_.refs_2_, bf16[1024,3072]{1,0:T(8,128)(2,1)} %get-tuple-element.178.refs_0_.refs_1_.refs_2_, ...), custom_call_target="tpu_custom_call" | custom-call | flops 5368709120 | bytes 2097152 | tf_op jit(solution)/shard_map/attend_back/pallas_call | solution.py:329
  226.5 3.9 collect_grads.6
  230.4 3.7 collective-permute-start.33
  234.1 14.7 %attend_back.6.refs_10_ = bf16[3,1024,1024]{2,1,0:T(8,128)(2,1)} custom-call(bf16[1024,3072]{1,0:T(8,128)(2,1)} %get-tuple-element.178.refs_0_.refs_1_.refs_2_, bf16[1024,3072]{1,0:T(8,128)(2,1)} %get-tuple-element.178.refs_0_.refs_1_.refs_2_, bf16[1024,3072]{1,0:T(8,128)(2,1)} %get-tuple-element.178.refs_0_.refs_1_.refs_2_, ...), custom_call_target="tpu_custom_call", output_to_operand_aliasing={{}: (10, {})} | custom-call | flops 10737418240 | bytes 4194304 | tf_op jit(solution)/shard_map/attend_back/pallas_call | solution.py:329
  248.9 5.9 %collect_grads.7 = (bf16[4,208,1024]{2,1,0:T(8,128)(2,1)}, bf16[4,208,1024]{2,1,0:T(8,128)(2,1)}) custom-call(s32[5,4]{1,0:T(8,128)} %concatenate.152.chosen_ref, bf16[32,176,1024]{2,1,0:T(8,128)(2,1)} %bitcast.134, bf16[32,176,1024]{2,1,0:T(8,128)(2,1)} %bitcast.135, bf16[32,176,1024]{2,1,0:T(8,128)(2,1)} %bitcast.136, bf16[32,176,1024]{2,1,0:T(8,128)(2,1)} %bitcast.137, ...), custom_call_target="tpu_custom_call" | custom-call | flops 10223616 | bytes 10223616 | tf_op jit(solution)/shard_map/collect_grads/pallas_call | solution.py:779
  256.9 14.9 %attend_back.7.refs_10_ = bf16[3,1024,1024]{2,1,0:T(8,128)(2,1)} custom-call(bf16[1024,3072]{1,0:T(8,128)(2,1)} %get-tuple-element.178.refs_0_.refs_1_.refs_2_, bf16[1024,3072]{1,0:T(8,128)(2,1)} %get-tuple-element.178.refs_0_.refs_1_.refs_2_, bf16[1024,3072]{1,0:T(8,128)(2,1)} %get-tuple-element.178.refs_0_.refs_1_.refs_2_, ...), custom_call_target="tpu_custom_call", output_to_operand_aliasing={{}: (10, {})} | custom-call | flops 10737418240 | bytes 4194304 | tf_op jit(solution)/shard_map/attend_back/pallas_call | solution.py:329
  271.8 3.5 collect_grads.8
  275.3 3.8 collective-permute-start.37
  279.1 15.0 %attend_back.8.refs_10_ = bf16[3,1024,1024]{2,1,0:T(8,128)(2,1)} custom-call(bf16[1024,3072]{1,0:T(8,128)(2,1)} %get-tuple-element.178.refs_0_.refs_1_.refs_2_, bf16[1024,3072]{1,0:T(8,128)(2,1)} %get-tuple-element.178.refs_0_.refs_1_.refs_2_, bf16[1024,3072]{1,0:T(8,128)(2,1)} %get-tuple-element.178.refs_0_.refs_1_.refs_2_, ...), custom_call_target="tpu_custom_call", output_to_operand_aliasing={{}: (10, {})} | custom-call | flops 10737418240 | bytes 4194304 | tf_op jit(solution)/shard_map/attend_back/pallas_call | solution.py:329
  295.2 5.0 %collect_grads.9 = bf16[4,208,1024]{2,1,0:T(8,128)(2,1)} custom-call(s32[5,4]{1,0:T(8,128)} %concatenate.152.chosen_ref, bf16[32,176,1024]{2,1,0:T(8,128)(2,1)} %bitcast.138, bf16[32,176,1024]{2,1,0:T(8,128)(2,1)} %bitcast.139, bf16[32,176,1024]{2,1,0:T(8,128)(2,1)} %bitcast.140, bf16[32,176,1024]{2,1,0:T(8,128)(2,1)} %bitcast.141, ...), custom_call_target="tpu_custom_call" | custom-call | flops 6815744 | bytes 6815744 | tf_op jit(solution)/shard_map/collect_grads/pallas_call | solution.py:779
  300.9 8.7 %attend_back.9.gp_ref.refs_9_ = bf16[3,1024,1024]{2,1,0:T(8,128)(2,1)} custom-call(bf16[1024,3072]{1,0:T(8,128)(2,1)} %get-tuple-element.178.refs_0_.refs_1_.refs_2_, bf16[1024,3072]{1,0:T(8,128)(2,1)} %get-tuple-element.178.refs_0_.refs_1_.refs_2_, bf16[1024,3072]{1,0:T(8,128)(2,1)} %get-tuple-element.178.refs_0_.refs_1_.refs_2_, ...), custom_call_target="tpu_custom_call", output_to_operand_aliasing={{}: (10, {})} | custom-call | flops 5368709120 | bytes 2097152 | tf_op jit(solution)/shard_map/attend_back/pallas_call | solution.py:329
  309.6 3.7 collect_last_grads.3
  316.8 13.6 %grad_qkv.1 = (bf16[1536,1024]{1,0:T(8,128)(2,1)}, bf16[1536,1024]{1,0:T(8,128)(2,1)}) custom-call(s32[1]{0:T(128)} %bitcast.120.core_ref, bf16[3,1024,1024]{2,1,0:T(8,128)(2,1)} %attend_back.9.gp_ref.refs_9_, bf16[1024,1024]{1,0:T(8,128)(2,1)} %get-tuple-element.242.hid_ref), custom_call_target="tpu_custom_call" | custom-call | flops 6442450944 | bytes 14680064 | tf_op jit(solution)/shard_map/grad_qkv/pallas_call | solution.py:567
  331.1 5.5 %collect_last_grads.4 = (bf16[208,1024]{1,0:T(8,128)(2,1)}, bf16[208,1024]{1,0:T(8,128)(2,1)}, f32[208,1024]{1,0:T(8,128)}, f32[208,1024]{1,0:T(8,128)}) custom-call(s32[5,4]{1,0:T(8,128)} %concatenate.152.chosen_ref, bf16[32,176,1024]{2,1,0:T(8,128)(2,1)} %bitcast.142, bf16[32,176,1024]{2,1,0:T(8,128)(2,1)} %bitcast.143, bf16[32,176,1024]{2,1,0:T(8,128)(2,1)} %bitcast.144, ...), custom_call_target="tpu_custom_call" | custom-call | flops 10223616 | bytes 10223616 | tf_op jit(solution)/shard_map/collect_last_grads/pallas_call | solution.py:779
  336.7 4.1 collect_grads.10
  344.0 3.8 collective-permute-start.43
  347.9 15.2 %grad_hidden_one.1.grad_ref = f32[1024,1024]{1,0:T(8,128)} custom-call(s32[32]{0:T(128)} %pad_add_fusion.3.refs_0_, bf16[4,104,1024]{2,1,0:T(8,128)(2,1)} %pad_maximum_fusion.1.refs_1_, bf16[4,104,1024]{2,1,0:T(8,128)(2,1)} %collective-permute-done.5.refs_2_, bf16[4,104,1024]{2,1,0:T(8,128)(2,1)} %collective-permute-done.10.refs_3_, ...), custom_call_target="tpu_custom_call" | custom-call | flops 6442450944 | bytes 16777216 | tf_op jit(solution)/shard_map/grad_hidden_one/pallas_call | solution.py:144
  363.0 4.1 collective-permute-done.44
  368.0 3.6 collect_grads.11
  379.7 7.3 %grad_tokens.1 = (f32[1024,1024]{1,0:T(8,128)}, f32[1,1024]{1,0:T(1,128)}) custom-call(f32[1024,1024]{1,0:T(8,128)} %grad_hidden_one.1.grad_ref, bf16[1024,1024]{1,0:T(8,128)(2,1)} %tok_ref.1, f32[1024,1024]{1,0:T(8,128)} %get-tuple-element.273.mid_ref, f32[2,1024]{1,0:T(2,128)} %get-tuple-element.202.refs_21_.gain_ref), custom_call_target="tpu_custom_call" | custom-call | flops 20971520 | bytes 14680064 | tf_op jit(solution)/shard_map/grad_tokens/pallas_call | solution.py:645
  389.1 3.7 all-to-all-start
  392.8 3.8 collect_last_grads.5
  403.1 12.6 %ffn_output.1 = bf16[1024,1024]{1,0:T(8,128)(2,1)} custom-call(s32[32]{0:T(128)} %pad_add_fusion.2.refs_1_.refs_0_, bf16[4,32,2816]{2,1,0:T(8,128)(2,1)} %pad_maximum_fusion.2.refs_10_.refs_1_, bf16[4,32,2816]{2,1,0:T(8,128)(2,1)} %collective-permute-done.16.refs_11_.refs_2_, bf16[4,32,2816]{2,1,0:T(8,128)(2,1)} %collective-permute-done.24.refs_12_.refs_3_, ...), custom_call_target="tpu_custom_call" | custom-call | flops 5905580032 | bytes 17825792 | tf_op jit(solution)/shard_map/ffn_output/pallas_call | solution.py:144
  (202 shorter events, 79.5 us)
Async XLA Ops:
  25.9 22.1 %collective-permute-start.5 = (bf16[4,104,1024]{2,1,0:T(8,128)(2,1)}, bf16[4,104,1024]{2,1,0:T(8,128)(2,1)}, u32[]{:S(2)}, u32[]{:S(2)}) collective-permute-start(bf16[4,104,1024]{2,1,0:T(8,128)(2,1)} %pad_maximum_fusion.1.refs_1_), channel_id=1, source_target_pairs={{0,4},{1,3},{2,6},{3,1},{4,0},{5,7},{6,2},{7,5},{8,12},{9,11},{10,... | collective-permute-start | bytes 2555912 | tf_op jit(solution)/shard_map/ppermute | solution.py:690
  26.4 21.6 %collective-permute-start.6 = (bf16[4,104,1024]{2,1,0:T(8,128)(2,1)}, bf16[4,104,1024]{2,1,0:T(8,128)(2,1)}, u32[]{:S(2)}, u32[]{:S(2)}) collective-permute-start(bf16[4,104,1024]{2,1,0:T(8,128)(2,1)} %pad_maximum_fusion.1.refs_1_), channel_id=1, source_target_pairs={{0,2},{1,5},{2,0},{3,7},{4,6},{5,1},{6,4},{7,3},{8,10},{9,13},{10,... | collective-permute-start | bytes 2555912 | tf_op jit(solution)/shard_map/ppermute | solution.py:690
  26.9 20.0 %collective-permute-start.9 = (bf16[32,2816]{1,0:T(8,128)(2,1)S(1)}, bf16[32,2816]{1,0:T(8,128)(2,1)S(1)}, u32[]{:S(2)}, u32[]{:S(2)}) collective-permute-start(bf16[32,2816]{1,0:T(8,128)(2,1)S(1)} %collective-permute-done.3), channel_id=1, source_target_pairs={{0,4},{1,3},{2,6},{3,1},{4,0},{5,7},{6,2},{7,5},{8,12},{9,11},{10,... | collective-permute-start | bytes 540680 | tf_op jit(solution)/shard_map/ppermute | solution.py:690
  28.4 19.5 %collective-permute-start.7 = (bf16[208,1024]{1,0:T(8,128)(2,1)S(1)}, bf16[208,1024]{1,0:T(8,128)(2,1)S(1)}, u32[]{:S(2)}, u32[]{:S(2)}) collective-permute-start(bf16[208,1024]{1,0:T(8,128)(2,1)S(1)} %fusion.1), channel_id=1, source_target_pairs={{0,8},{1,9},{2,10},{3,11},{4,12},{5,13},{6,14},{7,15},{8,16},{9,17... | collective-permute-start | bytes 1277960 | tf_op jit(solution)/shard_map/ppermute | solution.py:690
  28.4 19.5 %collective-permute-start.8 = (bf16[208,1024]{1,0:T(8,128)(2,1)S(1)}, bf16[208,1024]{1,0:T(8,128)(2,1)S(1)}, u32[]{:S(2)}, u32[]{:S(2)}) collective-permute-start(bf16[208,1024]{1,0:T(8,128)(2,1)S(1)} %fusion.1), channel_id=1, source_target_pairs={{0,24},{1,25},{2,26},{3,27},{4,28},{5,29},{6,30},{7,31},{8,0},{9,1... | collective-permute-start | bytes 1277960 | tf_op jit(solution)/shard_map/ppermute | solution.py:690
  47.9 17.4 %collective-permute-start.10 = (bf16[4,104,1024]{2,1,0:T(8,128)(2,1)}, bf16[4,104,1024]{2,1,0:T(8,128)(2,1)}, u32[]{:S(2)}, u32[]{:S(2)}) collective-permute-start(bf16[4,104,1024]{2,1,0:T(8,128)(2,1)} %collective-permute-done.5.refs_2_), channel_id=1, source_target_pairs={{0,2},{1,5},{2,0},{3,7},{4,6},{5,1},{6,4},{7,3},{8,10},{9,13},{10,... | collective-permute-start | bytes 2555912 | tf_op jit(solution)/shard_map/ppermute | solution.py:690
  66.1 20.6 %collective-permute-start.16 = (bf16[4,32,2816]{2,1,0:T(8,128)(2,1)}, bf16[4,32,2816]{2,1,0:T(8,128)(2,1)}, u32[]{:S(2)}, u32[]{:S(2)}) collective-permute-start(bf16[4,32,2816]{2,1,0:T(8,128)(2,1)} %pad_maximum_fusion.2.refs_10_.refs_1_), channel_id=1, source_target_pairs={{0,8},{1,9},{2,10},{3,11},{4,12},{5,13},{6,14},{7,15},{8,16},{9,17... | collective-permute-start | bytes 2162696 | tf_op jit(solution)/shard_map/ppermute | solution.py:690
  66.4 20.4 %collective-permute-start.17 = (bf16[4,32,2816]{2,1,0:T(8,128)(2,1)}, bf16[4,32,2816]{2,1,0:T(8,128)(2,1)}, u32[]{:S(2)}, u32[]{:S(2)}) collective-permute-start(bf16[4,32,2816]{2,1,0:T(8,128)(2,1)} %pad_maximum_fusion.2.refs_10_.refs_1_), channel_id=1, source_target_pairs={{0,1},{1,0},{2,3},{3,2},{4,5},{5,4},{6,7},{7,6},{8,9},{9,8},{10,11... | collective-permute-start | bytes 2162696 | tf_op jit(solution)/shard_map/ppermute | solution.py:694
  67.4 39.7 %collective-permute-start.18 = (bf16[4,208,1024]{2,1,0:T(8,128)(2,1)S(1)}, bf16[4,208,1024]{2,1,0:T(8,128)(2,1)}, u32[]{:S(2)}, u32[]{:S(2)}) collective-permute-start(bf16[4,208,1024]{2,1,0:T(8,128)(2,1)S(1)} %pad_maximum_fusion.refs_2_), channel_id=1, source_target_pairs={{0,4},{1,3},{2,6},{3,1},{4,0},{5,7},{6,2},{7,5},{8,12},{9,11},{10,... | collective-permute-start | bytes 5111816 | tf_op jit(solution)/shard_map/ppermute | solution.py:690
  67.7 39.3 %collective-permute-start.19 = (bf16[4,208,1024]{2,1,0:T(8,128)(2,1)S(1)}, bf16[4,208,1024]{2,1,0:T(8,128)(2,1)}, u32[]{:S(2)}, u32[]{:S(2)}) collective-permute-start(bf16[4,208,1024]{2,1,0:T(8,128)(2,1)S(1)} %pad_maximum_fusion.refs_2_), channel_id=1, source_target_pairs={{0,2},{1,5},{2,0},{3,7},{4,6},{5,1},{6,4},{7,3},{8,10},{9,13},{10,... | collective-permute-start | bytes 5111816 | tf_op jit(solution)/shard_map/ppermute | solution.py:690
  86.8 20.2 %collective-permute-start.21 = (bf16[4,208,1024]{2,1,0:T(8,128)(2,1)S(1)}, bf16[4,208,1024]{2,1,0:T(8,128)(2,1)}, u32[]{:S(2)}, u32[]{:S(2)}) collective-permute-start(bf16[4,208,1024]{2,1,0:T(8,128)(2,1)S(1)} %pad_maximum_fusion.refs_2_), channel_id=1, source_target_pairs={{0,1},{1,0},{2,3},{3,2},{4,5},{5,4},{6,7},{7,6},{8,9},{9,8},{10,11... | collective-permute-start | bytes 5111816 | tf_op jit(solution)/shard_map/ppermute | solution.py:694
  86.8 18.9 %collective-permute-start.20 = (bf16[4,32,2816]{2,1,0:T(8,128)(2,1)}, bf16[4,32,2816]{2,1,0:T(8,128)(2,1)}, u32[]{:S(2)}, u32[]{:S(2)}) collective-permute-start(bf16[4,32,2816]{2,1,0:T(8,128)(2,1)} %pad_maximum_fusion.2.refs_10_.refs_1_), channel_id=1, source_target_pairs={{0,24},{1,25},{2,26},{3,27},{4,28},{5,29},{6,30},{7,31},{8,0},{9,1... | collective-permute-start | bytes 2162696 | tf_op jit(solution)/shard_map/ppermute | solution.py:690
  107.0 22.0 %collective-permute-start.23 = (bf16[4,208,1024]{2,1,0:T(8,128)(2,1)}, bf16[4,208,1024]{2,1,0:T(8,128)(2,1)S(1)}, u32[]{:S(2)}, u32[]{:S(2)}) collective-permute-start(bf16[4,208,1024]{2,1,0:T(8,128)(2,1)} %collective-permute-done.18.refs_3_), channel_id=1, source_target_pairs={{0,2},{1,5},{2,0},{3,7},{4,6},{5,1},{6,4},{7,3},{8,10},{9,13},{10,... | collective-permute-start | bytes 5111816 | tf_op jit(solution)/shard_map/ppermute | solution.py:690
  107.5 21.6 %collective-permute-start.25 = (bf16[4,208,1024]{2,1,0:T(8,128)(2,1)}, bf16[4,208,1024]{2,1,0:T(8,128)(2,1)}, u32[]{:S(2)}, u32[]{:S(2)}) collective-permute-start(bf16[4,208,1024]{2,1,0:T(8,128)(2,1)} %collective-permute-done.18.refs_3_), channel_id=1, source_target_pairs={{0,1},{1,0},{2,3},{3,2},{4,5},{5,4},{6,7},{7,6},{8,9},{9,8},{10,11... | collective-permute-start | bytes 5111816 | tf_op jit(solution)/shard_map/ppermute | solution.py:694
  107.5 21.6 %collective-permute-start.26 = (bf16[4,208,1024]{2,1,0:T(8,128)(2,1)}, bf16[4,208,1024]{2,1,0:T(8,128)(2,1)}, u32[]{:S(2)}, u32[]{:S(2)}) collective-permute-start(bf16[4,208,1024]{2,1,0:T(8,128)(2,1)} %collective-permute-done.19.refs_5_), channel_id=1, source_target_pairs={{0,1},{1,0},{2,3},{3,2},{4,5},{5,4},{6,7},{7,6},{8,9},{9,8},{10,11... | collective-permute-start | bytes 5111816 | tf_op jit(solution)/shard_map/ppermute | solution.py:694
  108.0 20.4 %collective-permute-start.24 = (bf16[4,32,2816]{2,1,0:T(8,128)(2,1)}, bf16[4,32,2816]{2,1,0:T(8,128)(2,1)}, u32[]{:S(2)}, u32[]{:S(2)}) collective-permute-start(bf16[4,32,2816]{2,1,0:T(8,128)(2,1)} %collective-permute-done.16.refs_11_.refs_2_), channel_id=1, source_target_pairs={{0,8},{1,9},{2,10},{3,11},{4,12},{5,13},{6,14},{7,15},{8,16},{9,17... | collective-permute-start | bytes 2162696 | tf_op jit(solution)/shard_map/ppermute | solution.py:690
  108.0 20.4 %collective-permute-start.27 = (bf16[4,32,2816]{2,1,0:T(8,128)(2,1)}, bf16[4,32,2816]{2,1,0:T(8,128)(2,1)}, u32[]{:S(2)}, u32[]{:S(2)}) collective-permute-start(bf16[4,32,2816]{2,1,0:T(8,128)(2,1)} %collective-permute-done.20.refs_13_.refs_4_), channel_id=1, source_target_pairs={{0,1},{1,0},{2,3},{3,2},{4,5},{5,4},{6,7},{7,6},{8,9},{9,8},{10,11... | collective-permute-start | bytes 2162696 | tf_op jit(solution)/shard_map/ppermute | solution.py:694
  223.6 25.2 %collective-permute-start.31 = (bf16[32,176,1024]{2,1,0:T(8,128)(2,1)}, bf16[32,176,1024]{2,1,0:T(8,128)(2,1)}, u32[]{:S(2)}, u32[]{:S(2)}) collective-permute-start(bf16[32,176,1024]{2,1,0:T(8,128)(2,1)} %bitcast.133), channel_id=1, source_target_pairs={{0,1},{1,0},{2,3},{3,2},{4,5},{5,4},{6,7},{7,6},{8,9},{9,8},{10,11... | collective-permute-start | bytes 34603016 | tf_op jit(solution)/shard_map/ppermute | solution.py:694
  224.0 24.9 %collective-permute-start.32 = (bf16[32,32,1024]{2,1,0:T(8,128)(2,1)}, bf16[32,32,1024]{2,1,0:T(8,128)(2,1)}, u32[]{:S(2)}, u32[]{:S(2)}) collective-permute-start(bf16[32,32,1024]{2,1,0:T(8,128)(2,1)} %bitcast.171), channel_id=1, source_target_pairs={{0,1},{1,0},{2,3},{3,2},{4,5},{5,4},{6,7},{7,6},{8,9},{9,8},{10,11... | collective-permute-start | bytes 6291464 | tf_op jit(solution)/shard_map/ppermute | solution.py:694
  230.4 41.4 %collective-permute-start.33 = (bf16[4,32,2816]{2,1,0:T(8,128)(2,1)}, bf16[4,32,2816]{2,1,0:T(8,128)(2,1)}, u32[]{:S(2)}, u32[]{:S(2)}) collective-permute-start(bf16[4,32,2816]{2,1,0:T(8,128)(2,1)} %get-tuple-element.223), channel_id=1, source_target_pairs={{0,24},{1,25},{2,26},{3,27},{4,28},{5,29},{6,30},{7,31},{8,0},{9,1... | collective-permute-start | bytes 2162696 | tf_op jit(solution)/shard_map/ppermute | solution.py:690
  234.1 37.7 %collective-permute-start.34 = (bf16[4,32,2816]{2,1,0:T(8,128)(2,1)}, bf16[4,32,2816]{2,1,0:T(8,128)(2,1)}, u32[]{:S(2)}, u32[]{:S(2)}) collective-permute-start(bf16[4,32,2816]{2,1,0:T(8,128)(2,1)} %get-tuple-element.224), channel_id=1, source_target_pairs={{0,8},{1,9},{2,10},{3,11},{4,12},{5,13},{6,14},{7,15},{8,16},{9,17... | collective-permute-start | bytes 2162696 | tf_op jit(solution)/shard_map/ppermute | solution.py:690
  254.8 39.5 %collective-permute-start.35 = (bf16[4,208,1024]{2,1,0:T(8,128)(2,1)}, bf16[4,208,1024]{2,1,0:T(8,128)(2,1)}, u32[]{:S(2)}, u32[]{:S(2)}) collective-permute-start(bf16[4,208,1024]{2,1,0:T(8,128)(2,1)} %get-tuple-element.228), channel_id=1, source_target_pairs={{0,2},{1,5},{2,0},{3,7},{4,6},{5,1},{6,4},{7,3},{8,10},{9,13},{10,... | collective-permute-start | bytes 5111816 | tf_op jit(solution)/shard_map/ppermute | solution.py:690
  255.5 39.7 %collective-permute-start.36 = (bf16[4,208,1024]{2,1,0:T(8,128)(2,1)}, bf16[4,208,1024]{2,1,0:T(8,128)(2,1)S(1)}, u32[]{:S(2)}, u32[]{:S(2)}) collective-permute-start(bf16[4,208,1024]{2,1,0:T(8,128)(2,1)} %get-tuple-element.229), channel_id=1, source_target_pairs={{0,2},{1,5},{2,0},{3,7},{4,6},{5,1},{6,4},{7,3},{8,10},{9,13},{10,... | collective-permute-start | bytes 5111816 | tf_op jit(solution)/shard_map/ppermute | solution.py:690
  275.3 19.0 %collective-permute-start.37 = (bf16[4,32,2816]{2,1,0:T(8,128)(2,1)}, bf16[4,32,2816]{2,1,0:T(8,128)(2,1)}, u32[]{:S(2)}, u32[]{:S(2)}) collective-permute-start(bf16[4,32,2816]{2,1,0:T(8,128)(2,1)} %collect_grads.8), channel_id=1, source_target_pairs={{0,24},{1,25},{2,26},{3,27},{4,28},{5,29},{6,30},{7,31},{8,0},{9,1... | collective-permute-start | bytes 2162696 | tf_op jit(solution)/shard_map/ppermute | solution.py:690
  300.2 30.2 %collective-permute-start.38 = (bf16[4,208,1024]{2,1,0:T(8,128)(2,1)}, bf16[4,208,1024]{2,1,0:T(8,128)(2,1)}, u32[]{:S(2)}, u32[]{:S(2)}) collective-permute-start(bf16[4,208,1024]{2,1,0:T(8,128)(2,1)} %collect_grads.9), channel_id=1, source_target_pairs={{0,4},{1,3},{2,6},{3,1},{4,0},{5,7},{6,2},{7,5},{8,12},{9,11},{10,... | collective-permute-start | bytes 5111816 | tf_op jit(solution)/shard_map/ppermute | solution.py:690
  313.2 17.1 %collective-permute-start.39 = (bf16[32,2816]{1,0:T(8,128)(2,1)}, bf16[32,2816]{1,0:T(8,128)(2,1)S(1)}, u32[]{:S(2)}, u32[]{:S(2)}) collective-permute-start(bf16[32,2816]{1,0:T(8,128)(2,1)} %get-tuple-element.246), channel_id=1, source_target_pairs={{0,6},{1,7},{2,4},{3,5},{4,2},{5,3},{6,0},{7,1},{8,14},{9,15},{10,... | collective-permute-start | bytes 540680 | tf_op jit(solution)/shard_map/ppermute | solution.py:690
  340.8 26.3 %collective-permute-start.45 = (bf16[4,96,1024]{2,1,0:T(8,128)(2,1)}, bf16[4,96,1024]{2,1,0:T(8,128)(2,1)S(1)}, u32[]{:S(2)}, u32[]{:S(2)}) collective-permute-start(bf16[4,96,1024]{2,1,0:T(8,128)(2,1)} %get-tuple-element.264), channel_id=1, source_target_pairs={{0,2},{1,5},{2,0},{3,7},{4,6},{5,1},{6,4},{7,3},{8,10},{9,13},{10,... | collective-permute-start | bytes 2359304 | tf_op jit(solution)/shard_map/ppermute | solution.py:690
  342.4 24.7 %collective-permute-start.46 = (bf16[4,96,1024]{2,1,0:T(8,128)(2,1)}, bf16[4,96,1024]{2,1,0:T(8,128)(2,1)S(1)}, u32[]{:S(2)}, u32[]{:S(2)}) collective-permute-start(bf16[4,96,1024]{2,1,0:T(8,128)(2,1)} %get-tuple-element.265), channel_id=1, source_target_pairs={{0,2},{1,5},{2,0},{3,7},{4,6},{5,1},{6,4},{7,3},{8,10},{9,13},{10,... | collective-permute-start | bytes 2359304 | tf_op jit(solution)/shard_map/ppermute | solution.py:690
  344.0 19.0 %collective-permute-start.43 = (bf16[208,1024]{1,0:T(8,128)(2,1)}, bf16[208,1024]{1,0:T(8,128)(2,1)}, u32[]{:S(2)}, u32[]{:S(2)}) collective-permute-start(bf16[208,1024]{1,0:T(8,128)(2,1)} %get-tuple-element.261), channel_id=1, source_target_pairs={{0,24},{1,25},{2,26},{3,27},{4,28},{5,29},{6,30},{7,31},{8,0},{9,1... | collective-permute-start | bytes 1277960 | tf_op jit(solution)/shard_map/ppermute | solution.py:690
  347.9 19.2 %collective-permute-start.44 = (bf16[208,1024]{1,0:T(8,128)(2,1)}, bf16[208,1024]{1,0:T(8,128)(2,1)S(1)}, u32[]{:S(2)}, u32[]{:S(2)}) collective-permute-start(bf16[208,1024]{1,0:T(8,128)(2,1)} %get-tuple-element.262), channel_id=1, source_target_pairs={{0,8},{1,9},{2,10},{3,11},{4,12},{5,13},{6,14},{7,15},{8,16},{9,17... | collective-permute-start | bytes 1277960 | tf_op jit(solution)/shard_map/ppermute | solution.py:690
  389.1 26.7 %all-to-all-start = ((f32[32,2,32]{2,1,0:T(2,128)}), f32[32,2,32]{2,1,0:T(2,128)S(1)}, u32[]{:S(2)}, u32[]{:S(2)}) async-start(f32[32,2,32]{2,1,0:T(2,128)} %pad_maximum_fusion.5), calls=%async_computation | async-start | bytes 65536 | tf_op jit(solution)/shard_map/all_to_all | solution.py:968
  396.6 19.7 %collective-permute-start.49 = (bf16[96,1024]{1,0:T(8,128)(2,1)}, bf16[96,1024]{1,0:T(8,128)(2,1)S(1)}, u32[]{:S(2)}, u32[]{:S(2)}) collective-permute-start(bf16[96,1024]{1,0:T(8,128)(2,1)} %get-tuple-element.285), channel_id=1, source_target_pairs={{0,16},{1,17},{2,18},{3,19},{4,20},{5,21},{6,22},{7,23},{8,24},{9,... | collective-permute-start | bytes 589832 | tf_op jit(solution)/shard_map/ppermute | solution.py:690
  (49 other events, 451.0 us)
